TPU v7x, 512 devices: a whole 4x8x8 slice. The times are simulated.
512 devices in a mesh: seq: 32 (over z, y_hi), chan: 8 (over x, y_lo), dp: 2 (over core).
Axes of the slice: x: 4, y: 8 (y_hi: 4, y_lo: 2; y = y_hi * 2 + y_lo), z: 8, core: 2. Of those that a mesh axis runs over, the one named last changes fastest.
Arguments:
- hidden: bfloat16 [8192, 2048], P(('dp', 'seq')), parts along dimension 0, may hold values from -6 to 6
- complement: bfloat16 [8192, 2048], P(('dp', 'seq')), parts along dimension 0, may hold values from -6 to 6
- inner_weight: bfloat16 [2048, 4096], P(None, 'chan'), may hold values from -0.125 to 0.125
- select_weight: bfloat16 [2048, 256], replicated, may hold values from -0.015625 to 0.015625
- step_weight: bfloat16 [2048, 64], P(None, 'chan'), may hold values from -0.125 to 0.125
- step_bias: float32 [64], P('chan'), may hold values from -4 to -2
- decay_rate: float32 [64], P('chan'), as said below
- skip_gain: float32 [64], P('chan'), may hold values from 0.5 to 2
- cotangent: bfloat16 [8192, 4096], P(('dp', 'seq'), 'chan'), parts along dimension 0, may hold values from -6 to 6
- complement_cotangent: bfloat16 [8192, 4096], P(('dp', 'seq'), 'chan'), parts along dimension 0, may hold values from -6 to 6
Outputs:
- mixed: bfloat16 [8192, 4096], P(('dp', 'seq'), 'chan'), parts along dimension 0
- mixed_complement: bfloat16 [8192, 4096], P(('dp', 'seq'), 'chan'), parts along dimension 0
- grad_hidden: bfloat16 [8192, 2048], P(('dp', 'seq'), 'chan'), parts along dimension 0
- grad_complement: bfloat16 [8192, 2048], P(('dp', 'seq'), 'chan'), parts along dimension 0
There are 2 independent parts, one for each index of `dp`. A program takes and returns all parts, laid end to end along the dimension named above; an argument that names none is the same for every part. Nothing has to cross between parts.
Inputs may be any that keep to these rules, and one draw needn't show every extreme that they name: `decay_rate`: each head's decay rate lies between 7 / 4096 and 0.5.
All inputs are finite; a program needn't handle non-finite values.
Results may differ from a plain program's by a relative error of at most 0.006.
Values sent between devices are 32-bit elements; how exact they have to be, the bound alone decides.
A program may use at most 192 MiB of HBM per device.

v0:
```python
import jax
import jax.numpy as jnp
from jax import lax
from jax.sharding import PartitionSpec as P

highest = lax.Precision.HIGHEST


def carried_in(part, axis, combine, identity, reverse):
    count = lax.axis_size(axis)
    place = lax.axis_index(axis)
    ahead = count - 1 - place if reverse else place
    gathered = jax.tree.map(lambda a: lax.all_gather(a, axis), part)
    state = jax.tree.map(lambda a, e: jnp.zeros_like(a) + jnp.asarray(e, a.dtype), part, identity)

    def one(lap, state):
        source = count - 1 - lap if reverse else lap
        return combine(
            state, jax.tree.map(lambda a: lax.dynamic_index_in_dim(a, source, 0, False), gathered)
        )

    return lax.fori_loop(0, ahead, one, state)


def summary(values, write_keys, step_sizes, decay_rate):
    cumulative = jnp.cumsum(-step_sizes * decay_rate[None, :], axis=0)
    tail_weights = jnp.exp(cumulative[-1][None, :] - cumulative) * step_sizes
    state_out = jnp.einsum("sh,shp,sn->hpn", tail_weights, values, write_keys, precision=highest)
    return (state_out, cumulative[-1])


def response(values, write_keys, read_keys, step_sizes, decay_rate, state_in):
    cumulative = jnp.cumsum(-step_sizes * decay_rate[None, :], axis=0)
    length = values.shape[0]
    causal = lax.broadcasted_iota(jnp.int32, (length, length), 0) >= lax.broadcasted_iota(
        jnp.int32, (length, length), 1
    )
    cum_heads = cumulative.T
    log_gaps = cum_heads[:, :, None] - cum_heads[:, None, :]
    decays = jnp.exp(jnp.where(causal[None, :, :], log_gaps, -1e30))
    scores = jnp.dot(read_keys, write_keys.T, precision=highest)
    weights = decays * scores[None, :, :] * step_sizes.T[:, None, :]
    within = jnp.einsum("hts,shp->thp", weights, values, precision=highest)
    carried = jnp.exp(cumulative)[:, :, None] * jnp.einsum(
        "tn,hpn->thp", read_keys, state_in, precision=highest
    )
    return within + carried


def chain_combine(earlier, latter):
    return (earlier[0] * latter[0], latter[0][..., None, None] * earlier[1] + latter[1])


def carry_up(element):
    neutral = (jnp.ones_like(element[0]), jnp.zeros_like(element[1]))
    return carried_in(element, "seq", chain_combine, neutral, False)[1]


def carry_down(element):
    neutral = (jnp.ones_like(element[0]), jnp.zeros_like(element[1]))
    return carried_in(element, "seq", chain_combine, neutral, True)[1]


def local(
    hidden,
    complement,
    inner_weight,
    select_weight,
    step_weight,
    step_bias,
    decay_rate,
    skip_gain,
    cotangent,
    complement_cotangent,
):
    state_size = select_weight.shape[1] // 2
    local_heads = step_bias.shape[0]
    head_width = inner_weight.shape[1] // local_heads
    sources = jnp.stack([hidden, jnp.flip(complement, 1)])
    length = sources.shape[1]
    values = jnp.einsum(
        "srd,de->sre", sources, inner_weight, preferred_element_type=jnp.float32
    ).astype(jnp.bfloat16)
    keys = jnp.einsum(
        "srd,dn->srn", sources, select_weight, preferred_element_type=jnp.float32
    ).astype(jnp.bfloat16)
    raw_steps = jnp.einsum("srd,dh->srh", sources, step_weight, preferred_element_type=jnp.float32)
    step_sizes = jax.nn.softplus(raw_steps + step_bias[None, None, :])
    value_f = values.astype(jnp.float32).reshape(2, length, local_heads, head_width)
    write_f = keys[..., :state_size].astype(jnp.float32)
    read_f = keys[..., state_size:].astype(jnp.float32)

    def summaries(value_in, write_in, step_in):
        forward_part = jax.vmap(summary, (0, 0, 0, None))(value_in, write_in, step_in, decay_rate)
        backward_part = jax.vmap(summary, (0, 0, 0, None))(
            jnp.flip(value_in, 1), jnp.flip(write_in, 1), jnp.flip(step_in, 1), decay_rate
        )
        return (forward_part[0], forward_part[1], backward_part[0], backward_part[1])

    def mixer(value_in, write_in, read_in, step_in, state_fwd, state_bwd):
        forward_out = jax.vmap(response, (0, 0, 0, 0, None, 0))(
            value_in, write_in, read_in, step_in, decay_rate, state_fwd
        )
        backward_out = jax.vmap(response, (0, 0, 0, 0, None, 0))(
            jnp.flip(value_in, 1),
            jnp.flip(write_in, 1),
            jnp.flip(read_in, 1),
            jnp.flip(step_in, 1),
            decay_rate,
            state_bwd,
        )
        return forward_out + jnp.flip(backward_out, 1) + skip_gain[None, None, :, None] * value_in

    sums_out, sums_pullback = jax.vjp(summaries, value_f, write_f, step_sizes)
    decay_fwd = jnp.exp(sums_out[1])
    decay_bwd = jnp.exp(sums_out[3])
    state_fwd = carry_up((decay_fwd, sums_out[0]))
    state_bwd = carry_down((decay_bwd, sums_out[2]))
    mixed_f, mixer_pullback = jax.vjp(
        mixer, value_f, write_f, read_f, step_sizes, state_fwd, state_bwd
    )
    mixed_all = mixed_f.reshape(2, length, local_heads * head_width).astype(jnp.bfloat16)
    grad_mixed = (
        jnp.stack([cotangent, complement_cotangent])
        .astype(jnp.float32)
        .reshape(2, length, local_heads, head_width)
    )
    d_values, d_write, d_read, d_steps, grad_fwd, grad_bwd = mixer_pullback(grad_mixed)
    later_fwd = carry_down((decay_fwd, grad_fwd))
    later_bwd = carry_up((decay_bwd, grad_bwd))
    d_total_fwd = decay_fwd * jnp.sum(later_fwd * state_fwd, axis=(2, 3))
    d_total_bwd = decay_bwd * jnp.sum(later_bwd * state_bwd, axis=(2, 3))
    extra_values, extra_write, extra_steps = sums_pullback(
        (later_fwd, d_total_fwd, later_bwd, d_total_bwd)
    )
    value_grads = (
        (d_values + extra_values).reshape(2, length, local_heads * head_width).astype(jnp.bfloat16)
    )
    key_grads = jnp.concatenate([d_write + extra_write, d_read], axis=2)
    raw_grads = (d_steps + extra_steps) * jax.nn.sigmoid(raw_steps + step_bias[None, None, :])
    grad_term = jnp.einsum(
        "sre,de->srd", value_grads, inner_weight, preferred_element_type=jnp.float32
    )
    grad_term = grad_term + jnp.einsum(
        "srn,dn->srd", key_grads, select_weight.astype(jnp.float32), precision=highest
    )
    grad_term = grad_term + jnp.einsum(
        "srh,dh->srd", raw_grads, step_weight.astype(jnp.float32), precision=highest
    )
    grad_term = jnp.stack([grad_term[0], jnp.flip(grad_term[1], 1)])
    grad_shares = lax.psum_scatter(grad_term, "chan", scatter_dimension=2, tiled=True).astype(
        jnp.bfloat16
    )
    grad_first = grad_shares[0]
    grad_second = grad_shares[1]
    return (mixed_all[0], mixed_all[1], grad_first, grad_second)


def solution(mesh):
    in_specs = (
        P(("dp", "seq"), None),
        P(("dp", "seq"), None),
        P(None, "chan"),
        P(),
        P(None, "chan"),
        P("chan"),
        P("chan"),
        P("chan"),
        P(("dp", "seq"), "chan"),
        P(("dp", "seq"), "chan"),
    )
    out_specs = (
        P(("dp", "seq"), "chan"),
        P(("dp", "seq"), "chan"),
        P(("dp", "seq"), "chan"),
        P(("dp", "seq"), "chan"),
    )
    return jax.shard_map(local, mesh=mesh, in_specs=in_specs, out_specs=out_specs, check_vma=False)
```

profile of v0, /device:TPU:1, one launch (start us, length us, event | category | flops | bytes accessed | tf_op | source)
XLA Modules:
  0.0 1046.6 jit_solution(4561825273150341439)
XLA Ops:
  7.3 7.0 rev.56
  34.8 77.6 %all-gather.2 = f32[64,1,8]{2,1,0:T(1,128)} all-gather(f32[2,1,8]{2,1,0:T(1,128)S(1)} %bitcast.258), channel_id=4, replica_groups=mesh['seq'=32,'chan'=8,'dp'=2] {'seq'}, dimensions={0}, use_global_device_ids=true | all-gather | bytes 2112 | tf_op jit(solution)/shard_map/all_gather | solution.py:13
  112.9 69.7 %all-gather = f32[64,1,8]{2,1,0:T(1,128)} all-gather(f32[2,1,8]{2,1,0:T(1,128)S(1)} %bitcast.259), channel_id=2, replica_groups=mesh['seq'=32,'chan'=8,'dp'=2] {'seq'}, dimensions={0}, use_global_device_ids=true | all-gather | bytes 2112 | tf_op jit(solution)/shard_map/all_gather | solution.py:13
  182.6 66.9 %all-gather.15.cloned.1.call-done = f32[64,8,64,128]{3,2,1,0:T(8,128)} async-done(((f32[2,8,64,128]{3,2,1,0:T(8,128)}), f32[64,8,64,128]{3,2,1,0:T(8,128)}) %all-gather.15.cloned.1.call-update) | async-done | bytes 16777232 | tf_op jit(solution)/shard_map/all_gather | solution.py:13
  249.6 2.3 multiply_reduce_fusion.5
  252.7 213.0 %all-gather.17.cloned.1.call-done = f32[64,8,64,128]{3,2,1,0:T(8,128)} async-done(((f32[2,8,64,128]{3,2,1,0:T(8,128)}), f32[64,8,64,128]{3,2,1,0:T(8,128)}) %all-gather.17.cloned.1.call-update) | async-done | bytes 16777232 | tf_op jit(solution)/shard_map/all_gather | solution.py:13
  465.7 57.9 %while.55 = (s32[]{:T(128)}, f32[2,8,64,128]{3,2,1,0:T(8,128)S(1)}, s32[]{:T(128)}, f32[32,2,8]{2,1,0:T(2,128)}, f32[32,2,8,64,128]{4,3,2,1,0:T(8,128)}, /*index=5*/s32[]{:T(128)}, s32[]{:T(128)}, s32[]{:T(128)}, s32[]{:T(128)}) while((s32[]{:T(128)}, f32[2,8,64,128]{3,2,1,0:T(8,128)S(1)}, s32[]{:T(128)}, f32[32,2,8]{2,1,0:T(2,128)}, ...), condition=%wide.region_9.10_spmd, body=%wide.region_8.9_spmd.sunk | while | flops 262150 | bytes 1573203 | solution.py:22
  526.4 3.0 fusion.136
  530.3 2.0 fusion.71
  542.5 2.3 fusion.79
  544.8 137.3 %all-gather.13.cloned.1.call-done = f32[64,8,64,128]{3,2,1,0:T(8,128)} async-done(((f32[2,8,64,128]{3,2,1,0:T(8,128)}), f32[64,8,64,128]{3,2,1,0:T(8,128)}) %all-gather.13.cloned.1.call-update) | async-done | bytes 16777232 | tf_op jit(solution)/shard_map/all_gather | solution.py:13
  683.0 87.0 %while.53 = (s32[]{:T(128)}, f32[2,8,64,128]{3,2,1,0:T(8,128)}, s32[]{:T(128)}, f32[32,2,8]{2,1,0:T(2,128)}, f32[32,2,8,64,128]{4,3,2,1,0:T(8,128)}, /*index=5*/s32[]{:T(128)}, s32[]{:T(128)}, s32[]{:T(128)}, s32[]{:T(128)}) while((s32[]{:T(128)}, f32[2,8,64,128]{3,2,1,0:T(8,128)}, s32[]{:T(128)}, f32[32,2,8]{2,1,0:T(2,128)}, ...), condition=%wide.region_5.6_spmd, body=%wide.region_4.5_spmd.sunk | while | flops 262150 | bytes 1573203 | solution.py:22
  683.6 2.1 bitcast_add_fusion.13
  686.3 2.1 bitcast_add_fusion.13
  689.1 2.1 bitcast_add_fusion.13
  691.9 2.1 bitcast_add_fusion.13
  694.7 2.2 bitcast_add_fusion.13
  697.5 2.1 bitcast_add_fusion.13
  700.3 2.1 bitcast_add_fusion.13
  703.1 2.1 bitcast_add_fusion.13
  705.9 2.1 bitcast_add_fusion.13
  708.7 2.1 bitcast_add_fusion.13
  711.5 2.1 bitcast_add_fusion.13
  714.2 2.1 bitcast_add_fusion.13
  717.0 2.1 bitcast_add_fusion.13
  719.8 2.1 bitcast_add_fusion.13
  722.6 2.1 bitcast_add_fusion.13
  725.4 2.1 bitcast_add_fusion.13
  728.2 2.1 bitcast_add_fusion.13
  730.9 2.1 bitcast_add_fusion.13
  733.7 2.1 bitcast_add_fusion.13
  736.5 2.1 bitcast_add_fusion.13
  739.2 2.1 bitcast_add_fusion.13
  742.0 2.4 bitcast_add_fusion.13
  745.1 2.1 bitcast_add_fusion.13
  747.9 2.1 bitcast_add_fusion.13
  750.7 2.1 bitcast_add_fusion.13
  753.5 2.1 bitcast_add_fusion.13
  756.2 2.1 bitcast_add_fusion.13
  759.0 2.2 bitcast_add_fusion.13
  761.8 2.1 bitcast_add_fusion.13
  764.6 2.1 bitcast_add_fusion.13
  767.4 2.1 bitcast_add_fusion.13
  775.1 5.5 fusion.29
  783.5 3.2 convolution_bitcast_fusion.1
  786.7 2.1 rev.63
  788.8 2.1 rev.64
  794.5 2.7 convolution_bitcast_fusion.7
  798.8 2.2 convolution_bitcast_fusion.5
  804.4 3.8 reduce_window_sum.52
  808.2 2.1 fusion.15
  812.2 3.1 multiply_reduce_fusion.9
  817.1 81.5 %all-gather.11.cloned.1.call-done = f32[64,8,64,128]{3,2,1,0:T(8,128)} async-done(((f32[2,8,64,128]{3,2,1,0:T(8,128)}), f32[64,8,64,128]{3,2,1,0:T(8,128)}) %all-gather.11.cloned.1.call-update) | async-done | bytes 16777232 | tf_op jit(solution)/shard_map/all_gather | solution.py:13
  899.0 2.3 multiply_reduce_fusion.8
  904.0 2.0 fusion.16
  907.1 2.2 reduce_window_sum.50
  909.4 2.2 reduce_window_sum.51
  911.6 2.2 reduce_window_sum.53
  913.8 2.3 fusion.17
  920.5 5.9 rev.70
  926.4 3.1 pad_maximum_fusion
  930.7 3.8 fusion.5
  935.7 2.4 fusion.13
  939.7 98.5 %reduce-scatter.2.cloned.1.call-done = f32[2,128,256]{2,1,0:T(8,128)} async-done(((f32[2,128,2048]{2,1,0:T(8,128)}), f32[2,128,256]{2,1,0:T(8,128)}) %reduce-scatter.2.cloned.1.call-update) | async-done | bytes 262160 | tf_op jit(solution)/shard_map/reduce_scatter | solution.py:151
  (301 shorter events, 147.5 us)
Async XLA Ops:
  7.2 23.7 %copy-start = (bf16[2048,512]{1,0:T(8,128)(2,1)S(1)}, bf16[2048,512]{1,0:T(8,128)(2,1)}, u32[]{:S(2)}) copy-start(bf16[2048,512]{1,0:T(8,128)(2,1)} %param.20) | copy-start | bytes 6291460
  7.2 8.9 copy-start.55
  7.2 8.9 copy-start.47
  7.2 242.3 %all-gather.15.cloned.1.call-start = ((), (), s32[]{:S(2)}) async-start(), calls=%async_computation.4 | async-start | bytes 17301504 | tf_op jit(solution)/shard_map/all_gather | solution.py:13
  14.3 5.6 copy-start.22
  16.1 1.1 copy-start.15
  17.1 13.2 %copy-start.14 = (f32[2,128,8]{2,0,1:T(2,128)}, f32[2,128,8]{2,0,1:T(2,128)S(1)}, u32[]{:S(2)}) copy-start(f32[2,128,8]{2,0,1:T(2,128)S(1)} %get-tuple-element.341) | copy-start | bytes 24580
  17.2 2.8 copy-start.31
  17.5 0.6 copy-start.37
  18.1 5.3 copy-start.33
  19.9 7.7 copy-start.13
  20.0 4.8 copy-start.11
  20.2 7.4 copy-start.7
  21.3 6.3 copy-start.9
  23.4 7.1 copy-start.4
  24.8 440.9 %all-gather.17.cloned.1.call-start = ((), (), s32[]{:S(2)}) async-start(), calls=%async_computation.5 | async-start | bytes 17301504 | tf_op jit(solution)/shard_map/all_gather | solution.py:13
  27.5 7.1 copy-start.5
  27.6 2.7 copy-start.39
  27.6 0.6 copy-start.35
  29.4 652.7 %all-gather.13.cloned.1.call-start = ((), (), s32[]{:S(2)}) async-start(), calls=%async_computation.3 | async-start | bytes 17301504 | tf_op jit(solution)/shard_map/all_gather | solution.py:13
  29.6 0.7 copy-start.29
  30.3 0.6 copy-start.44
  30.8 2.3 copy-start.12
  33.1 216.4 %copy-start.2 = (f32[2,128,8,64]{1,3,2,0:T(8,128)}, f32[2,128,8,64]{1,3,2,0:T(8,128)S(1)}, u32[]{:S(2)}) copy-start(f32[2,128,8,64]{1,3,2,0:T(8,128)S(1)} %rev.57) | copy-start | bytes 1572868
  34.6 864.0 %all-gather.11.cloned.1.call-start = ((), (), s32[]{:S(2)}) async-start(), calls=%async_computation.2 | async-start | bytes 17301504 | tf_op jit(solution)/shard_map/all_gather | solution.py:13
  34.8 214.8 %copy-start.28 = (f32[2,128,8]{2,0,1:T(2,128)}, f32[2,128,8]{2,0,1:T(2,128)S(1)}, u32[]{:S(2)}) copy-start(f32[2,128,8]{2,0,1:T(2,128)S(1)} %copy.163) | copy-start | bytes 24580
  532.4 505.8 %reduce-scatter.2.cloned.1.call-start = ((), (), s32[]{:S(2)}) async-start(), calls=%async_computation.1 | async-start | bytes 2359296 | tf_op jit(solution)/shard_map/reduce_scatter | solution.py:151
  797.2 15.0 %copy-start.1 = (f32[2,8,64,128]{3,2,1,0:T(8,128)S(1)}, f32[2,8,64,128]{3,2,1,0:T(8,128)}, u32[]{:S(2)}) copy-start(f32[2,8,64,128]{3,2,1,0:T(8,128)} %get-tuple-element.261) | copy-start | bytes 1572868
  801.0 14.4 %copy-start.49 = (f32[2,8,128]{2,1,0:T(8,128)S(1)}, f32[2,8,128]{2,1,0:T(8,128)}, u32[]{:S(2)}) copy-start(f32[2,8,128]{2,1,0:T(8,128)} %copy.159) | copy-start | bytes 24580
  808.1 7.2 copy-start.8
  808.1 7.2 copy-start.10
  808.1 7.2 copy-start.21
  808.1 7.2 copy-start.23
  808.2 7.2 copy-start.24
  808.2 7.2 copy-start.32
  808.2 7.2 copy-start.43
  808.2 7.2 copy-start.50
  808.2 7.2 copy-start.57
  898.9 3.1 copy-start.38
  898.9 3.0 copy-start.40
  898.9 3.0 copy-start.42
  898.9 3.0 copy-start.51
  898.9 3.0 copy-start.52
  899.0 3.0 copy-start.53
  899.0 3.0 copy-start.54
  899.0 5.0 copy-start.36
  907.1 9.0 copy-start.27
  916.2 0.9 copy-start.18
  916.2 1.0 copy-start.25
  916.2 1.0 copy-start.26
  916.2 1.0 copy-start.45
  916.2 1.0 copy-start.48
  916.2 1.4 copy-start.6
  916.2 1.4 copy-start.16
  916.2 1.4 copy-start.17
  916.2 1.4 copy-start.19
  916.3 1.4 copy-start.46
  916.3 1.4 copy-start.56
  917.2 0.9 copy-start.41
  929.5 1.0 copy-start.3
  929.5 1.2 copy-start.20
  929.5 1.2 copy-start.30
  929.5 1.2 copy-start.34
Sparse Core Ops, SparseCore 0:
  24.9 224.5 all-gather.14
  252.7 212.9 all-gather.16
  468.8 213.2 all-gather.12
  685.1 213.4 all-gather.10
  929.6 108.5 reduce-scatter.1
where the time goes:
time: 1060 us; the launch traced here: 1050 us
  waiting for transfers between devices  597 us (56%)
  blocking collectives  147 us (14%)
  other arithmetic  132 us (12%)
  local copies, waits for them, and re-layouts  88.7 us (8%)
  matrix products  64.1 us (6%)
  between operations  15 us (1%)
    all_gather x4, waiting for transfers between devices, carried_in(): gathered = jax.tree.map(lambda a: lax.all_gather(a, axis), part)  499 us
    all_gather x2, blocking collectives, carried_in(): gathered = jax.tree.map(lambda a: lax.all_gather(a, axis), part)  147 us
    add x62, other arithmetic, chain_combine(): latter[0][..., None, None] * earlier[1] + latter[1]  103 us
    reduce_scatter x1, waiting for transfers between devices, local(): lax.psum_scatter(grad_term, 'chan', scatter_dimension=2, tiled=True)  98.5 us
    mul x62, local copies, waits for them, and re-layouts, chain_combine(): latter[0][..., None, None] * earlier[1] + latter[1]  40.3 us
  transfers between devices with their start and end apart: 5, of which 5 were waited for; matrix products, arithmetic and copies ran while one was open for 22% of the time, Pallas kernels for 0%

commit v1 on v0

v1 whole, which is shorter than its diff:
```python
import functools

import jax
import jax.numpy as jnp
from jax import lax
from jax.experimental import pallas as pl
from jax.experimental.pallas import tpu as pltpu
from jax.sharding import PartitionSpec as P

F32 = jnp.float32
BF16 = jnp.bfloat16
HIGHEST = lax.Precision.HIGHEST
HEAD = 64
STATE = 128
ROWS = 128
FLIP = 256
LANES = 128


def dot(a, b, ca=1, cb=0, precision=None):
    return lax.dot_general(
        a, b, (((ca,), (cb,)), ((), ())), precision=precision, preferred_element_type=F32
    )


def split(a):
    high = a.astype(BF16)
    return high, (a - high.astype(F32)).astype(BF16)


def dot_left(a, b, ca=1, cb=0):
    high, low = split(a)
    return dot(high, b, ca, cb) + dot(low, b, ca, cb)


def dot_right(a, b, ca=1, cb=0):
    high, low = split(b)
    return dot(a, high, ca, cb) + dot(a, low, ca, cb)


def dot_both(a, b, ca=1, cb=0):
    a_high, a_low = split(a)
    b_high, b_low = split(b)
    return dot(a_high, b_high, ca, cb) + (dot(a_high, b_low, ca, cb) + dot(a_low, b_high, ca, cb))


def iota(shape, dim):
    return lax.broadcasted_iota(jnp.int32, shape, dim)


def where01(mask, dtype=F32):
    return jnp.where(mask, 1.0, 0.0).astype(dtype)


def anti_identity():
    return where01(iota((FLIP, FLIP), 0) + iota((FLIP, FLIP), 1) == FLIP - 1, BF16)


def spread_matrix(channels):
    lanes = iota((LANES, channels), 1)
    row = iota((LANES, channels), 0) * HEAD
    return where01((lanes >= row) & (lanes < row + HEAD))


def decay_parts(dt, rate):
    log_decay = -dt * rate
    strict = where01(iota((ROWS, ROWS), 0) > iota((ROWS, ROWS), 1))
    before = dot(strict, log_decay, precision=HIGHEST)
    upto = before + log_decay
    total = upto[ROWS - 1 : ROWS, :]
    return log_decay, before, upto, total


def project_kernel(
    hidden, complement, inner, select, step, params, cot, ccot, send, values, keys, dts, sigs, source, step_wide
):
    channels = inner.shape[1]
    heads = channels // HEAD
    bias, rate = params[0:1, :], params[1:2, :]
    depth = hidden.shape[1]
    blocks = depth // FLIP
    source[:ROWS, :] = hidden[...]
    anti = anti_identity()
    for b in range(blocks):
        block = complement[:, (blocks - 1 - b) * FLIP : (blocks - b) * FLIP]
        source[ROWS:, b * FLIP : (b + 1) * FLIP] = dot(block, anti).astype(BF16)
    src = source[...]
    v_all = dot(src, inner[...]).astype(BF16)
    k_all = dot(src, select[...]).astype(BF16)
    step_wide[...] = jnp.zeros_like(step_wide)
    step_wide[:, :heads] = step[...]
    raw = dot(src, step_wide[...]) + bias
    small = jnp.exp(-jnp.abs(raw))
    one_more = 1.0 + small
    tail = jnp.where(
        one_more == 1.0, small, jnp.log(one_more) * (small / jnp.where(one_more == 1.0, 1.0, one_more - 1.0))
    )
    dt_all = jnp.maximum(raw, 0.0) + tail
    values[...] = v_all
    keys[...] = k_all
    dts[...] = dt_all
    sigs[...] = jnp.where(raw >= 0.0, 1.0, small) / one_more
    spread = spread_matrix(channels)
    ones = jnp.ones((ROWS, STATE), F32)
    for s in range(2):
        rows = slice(s * ROWS, (s + 1) * ROWS)
        dt = dt_all[rows]
        log_decay, before, upto, total = decay_parts(dt, rate)
        x = v_all[rows].astype(F32)
        g = (cot if s == 0 else ccot)[...].astype(F32)
        write, read = k_all[rows, :STATE], k_all[rows, STATE:]
        widen = lambda w: dot(w, spread, precision=HIGHEST)
        pieces = (
            (0, 0, widen(jnp.exp(total - upto) * dt) * x, write),
            (0, HEAD, widen(jnp.exp(total - before)) * g, read),
            (1, 0, widen(jnp.exp(before) * dt) * x, write),
            (1, HEAD, widen(jnp.exp(upto)) * g, read),
        )
        for way, at, left, right in pieces:
            state = dot_left(left, right, 0, 0)
            first = (way * 2 + s) * heads
            send[first : first + heads, at : at + HEAD, :] = state.reshape(heads, HEAD, STATE)
        decay = jnp.exp(dot(log_decay, ones, 0, 0, precision=HIGHEST))
        for way in range(2):
            for h in range(heads):
                send[(way * 2 + s) * heads + h, 2 * HEAD :, :] = jnp.broadcast_to(decay[h : h + 1], (8, STATE))


def scan_kernel(shards, arrived, back):
    mine = arrived.shape[0] // shards
    me = lax.axis_index("seq")
    for j in range(mine):
        down = (me * mine + j) // (shards * mine // 2)

        def one(lap, state):
            c = lap + down * (shards - 1 - 2 * lap)
            at = c * mine + j
            back[at] = state.reshape(2 * HEAD, STATE)
            part = arrived[at]
            decay = part[2 * HEAD :]
            return state * decay[None] + part[: 2 * HEAD].reshape(2 * HEAD // 8, 8, STATE)

        lax.fori_loop(0, shards, one, jnp.zeros((2 * HEAD // 8, 8, STATE), F32))


def finish_kernel(
    entry,
    values,
    keys,
    dts,
    sigs,
    inner,
    select,
    step,
    params,
    cot,
    ccot,
    mixed,
    cmixed,
    term,
    d_val,
    d_key,
    d_raw,
    step_wide,
):
    channels = values.shape[1]
    heads = channels // HEAD
    rate, skip = params[1:2, :], params[2:3, :]
    step_wide[...] = jnp.zeros_like(step_wide)
    step_wide[:, :heads] = step[...]
    spread = spread_matrix(channels)
    row_id, col_id = iota((ROWS, ROWS), 0), iota((ROWS, ROWS), 1)
    diagonal, lower, upper = row_id == col_id, row_id > col_id, row_id < col_id
    eye = where01(diagonal)
    twice = jnp.where(diagonal, 2.0, 1.0)
    lane_first = where01(iota((1, 2 * HEAD), 1) < HEAD, BF16)
    lane_second = where01(iota((1, 2 * HEAD), 1) >= HEAD, BF16)
    head_lane = iota((ROWS, LANES), 1)
    head_row = iota((heads, ROWS), 0)
    widen = lambda w: dot(w, spread, precision=HIGHEST)
    narrow = lambda w: dot(w, spread, 1, 1, precision=HIGHEST)
    skip_wide = widen(skip)
    for s in range(2):
        rows = slice(s * ROWS, (s + 1) * ROWS)
        dt = dts[rows, :]
        log_decay, before, upto, total = decay_parts(dt, rate)
        dt_t = dot(dt, eye, 0, 0, precision=HIGHEST)
        before_t = dot(log_decay, where01(upper), 0, 0, precision=HIGHEST)
        upto_t = before_t + dot(log_decay, eye, 0, 0, precision=HIGHEST)
        x_b, g_b = values[rows, :], (cot if s == 0 else ccot)[...]
        x, g = x_b.astype(F32), g_b.astype(F32)
        write, read = keys[rows, :STATE], keys[rows, STATE:]
        u_fwd, u_bwd = widen(jnp.exp(total - upto)), widen(jnp.exp(before))
        w_fwd, w_bwd = widen(jnp.exp(upto)), widen(jnp.exp(total - before))
        dt_wide = widen(dt)
        state = lambda way, at: entry[
            (way * 2 + s) * heads : (way * 2 + s + 1) * heads, at : at + HEAD, :
        ].reshape(heads * HEAD, STATE)
        h_in, m_in, k_in, l_in = state(0, 0), state(0, HEAD), state(1, 0), state(1, HEAD)
        y_fwd = w_fwd * dot_right(read, h_in, 1, 1)
        y_bwd = w_bwd * dot_right(read, k_in, 1, 1)
        x_l = u_fwd * dot_right(write, l_in, 1, 1)
        x_m = u_bwd * dot_right(write, m_in, 1, 1)
        d_read = dot_both(w_fwd * g, h_in) + dot_both(w_bwd * g, k_in)
        d_write = dot_both(u_fwd * dt_wide * x, l_in) + dot_both(u_bwd * dt_wide * x, m_in)
        r_fwd, r_bwd = narrow(g * y_fwd), narrow(g * y_bwd)
        q_fwd, q_bwd = narrow(x * x_l), narrow(x * x_m)
        both = dot(spread, l_in * h_in + m_in * k_in, precision=HIGHEST)
        both = dot(jnp.ones((8, STATE), F32), both, 1, 1, precision=HIGHEST)[0:1]
        scores = dot(read, write, 1, 1)
        d_scores = jnp.zeros((ROWS, ROWS), F32)
        by_row = jnp.zeros((ROWS, LANES), F32)
        by_row_up = jnp.zeros((ROWS, LANES), F32)
        direct_t = jnp.zeros((heads, ROWS), F32)
        low_t = jnp.zeros((heads, ROWS), F32)
        up_t = jnp.zeros((heads, ROWS), F32)
        for pair in range(heads // 2):
            lanes = slice(pair * 2 * HEAD, (pair + 1) * 2 * HEAD)
            x_pair, g_pair = x_b[:, lanes], g_b[:, lanes]
            y_pair = jnp.zeros((ROWS, 2 * HEAD), F32)
            d_pair = jnp.zeros((ROWS, 2 * HEAD), F32)
            for half, lane_mask in ((0, lane_first), (1, lane_second)):
                h = pair * 2 + half
                x_h, g_h = x_pair * lane_mask, g_pair * lane_mask
                gap = jnp.where(
                    upper,
                    before_t[h : h + 1, :] - before[:, h : h + 1],
                    upto[:, h : h + 1] - upto_t[h : h + 1, :],
                )
                decay = jnp.exp(jnp.minimum(gap, 0.0)) * twice
                dt_row = dt_t[h : h + 1, :]
                scaled = scores * decay
                weights = scaled * dt_row
                w_high, w_low = split(weights)
                y_pair = y_pair + (dot(w_high, x_h) + dot(w_low, x_h))
                d_pair = d_pair + (dot(w_high, g_h, 0, 0) + dot(w_low, g_h, 0, 0))
                outer = dot(g_h, x_pair, 1, 1)
                grads = outer * scaled
                d_scores = d_scores + outer * (decay * dt_row)
                q = grads * dt_row
                q_low, q_up = jnp.where(lower, q, 0.0), jnp.where(upper, q, 0.0)
                by_row = jnp.where(head_lane == h, jnp.sum(q_low, 1, keepdims=True), by_row)
                by_row_up = jnp.where(head_lane == h, jnp.sum(q_up, 1, keepdims=True), by_row_up)
                direct_t = jnp.where(head_row == h, jnp.sum(grads, 0, keepdims=True), direct_t)
                low_t = jnp.where(head_row == h, jnp.sum(q_low, 0, keepdims=True), low_t)
                up_t = jnp.where(head_row == h, jnp.sum(q_up, 0, keepdims=True), up_t)
            out = y_pair + y_fwd[:, lanes] + y_bwd[:, lanes] + skip_wide[:, lanes] * x[:, lanes]
            (mixed if s == 0 else cmixed)[:, lanes] = out.astype(BF16)
            grad = d_pair + dt_wide[:, lanes] * (x_l[:, lanes] + x_m[:, lanes])
            grad = grad + skip_wide[:, lanes] * g[:, lanes]
            d_val[rows, lanes] = grad.astype(BF16)
        stacked = (direct_t, low_t, up_t, jnp.zeros((ROWS - 3 * heads, ROWS), F32))
        turned = jnp.transpose(jnp.concatenate(stacked, 0))
        picked = lambda at: jnp.where(head_lane < heads, pltpu.roll(turned, LANES - at, 1) if at else turned, 0.0)
        d_dt = picked(0) + q_fwd + q_bwd
        d_upto = by_row - picked(heads) + r_fwd - dt * q_fwd
        d_before = picked(2 * heads) - by_row_up - r_bwd + dt * q_bwd
        d_total = jnp.sum(r_bwd + dt * q_fwd, 0, keepdims=True) + jnp.exp(total) * both
        from_here = where01(row_id <= col_id)
        d_log = dot(from_here, d_upto, precision=HIGHEST) + dot(where01(upper), d_before, precision=HIGHEST)
        d_log = d_log + d_total
        d_raw[rows, :] = (d_dt - rate * d_log) * sigs[rows, :]
        d_key[rows, :STATE] = d_write + dot_left(d_scores, read, 0, 0)
        d_key[rows, STATE:] = d_read + dot_left(d_scores, write)
    chunks = term.shape[0]
    width = term.shape[2]
    val = d_val[...]
    key_high, key_low = split(d_key[...])
    raw_high, raw_low = split(d_raw[...])
    for j in range(chunks):
        cols = slice(j * width, (j + 1) * width)
        part = dot(val, inner[cols, :], 1, 1)
        sel, stp = select[cols, :], step_wide[cols, :]
        part = part + (dot(key_high, sel, 1, 1) + dot(key_low, sel, 1, 1))
        part = part + (dot(raw_high, stp, 1, 1) + dot(raw_low, stp, 1, 1))
        term[j, :ROWS, :] = part[:ROWS]
        term[chunks - 1 - j, ROWS:, :] = part[ROWS:]


def combine_kernel(shares, first, second):
    total = shares[0]
    for j in range(1, shares.shape[0]):
        total = total + shares[j]
    total = total.astype(BF16)
    first[...] = total[:ROWS]
    anti = anti_identity()
    blocks = total.shape[1] // FLIP
    for b in range(blocks):
        block = total[ROWS:, (blocks - 1 - b) * FLIP : (blocks - b) * FLIP]
        second[:, b * FLIP : (b + 1) * FLIP] = dot(block, anti).astype(BF16)


def call(kernel, outs, args, scratch=()):
    whole = pl.BlockSpec(memory_space=pltpu.VMEM)
    return pl.pallas_call(
        kernel,
        out_shape=[jax.ShapeDtypeStruct(shape, dtype) for shape, dtype in outs],
        in_specs=[whole] * len(args),
        out_specs=[whole] * len(outs),
        scratch_shapes=[pltpu.VMEM(shape, dtype) for shape, dtype in scratch],
        compiler_params=pltpu.CompilerParams(vmem_limit_bytes=48 << 20),
    )(*args)


def local(hidden, complement, inner, select, step, bias, rate, skip, cot, ccot):
    shards, ranks = lax.axis_size("seq"), lax.axis_size("chan")
    heads = bias.shape[0]
    depth = hidden.shape[1]
    channels = heads * HEAD
    params = jnp.pad(jnp.stack([bias, rate, skip]), ((0, 5), (0, LANES - heads)))
    send, values, keys, dts, sigs = call(
        project_kernel,
        [
            ((4 * heads, 2 * HEAD + 8, STATE), F32),
            ((2 * ROWS, channels), BF16),
            ((2 * ROWS, 2 * STATE), BF16),
            ((2 * ROWS, LANES), F32),
            ((2 * ROWS, LANES), F32),
        ],
        (hidden, complement, inner, select, step, params, cot, ccot),
        [((2 * ROWS, depth), BF16), ((depth, LANES), BF16)],
    )
    arrived = lax.all_to_all(send, "seq", 0, 0, tiled=True)
    (back,) = call(
        functools.partial(scan_kernel, shards), [((4 * heads, 2 * HEAD, STATE), F32)], (arrived,)
    )
    entry = lax.all_to_all(back, "seq", 0, 0, tiled=True)
    mixed, cmixed, term = call(
        finish_kernel,
        [
            ((ROWS, channels), BF16),
            ((ROWS, channels), BF16),
            ((ranks, 2 * ROWS, depth // ranks), F32),
        ],
        (entry, values, keys, dts, sigs, inner, select, step, params, cot, ccot),
        [
            ((2 * ROWS, channels), BF16),
            ((2 * ROWS, 2 * STATE), F32),
            ((2 * ROWS, LANES), F32),
            ((depth, LANES), BF16),
        ],
    )
    shares = lax.all_to_all(term, "chan", 0, 0, tiled=True)
    first, second = call(combine_kernel, [((ROWS, depth // ranks), BF16)] * 2, (shares,))
    return mixed, cmixed, first, second


def solution(mesh):
    rows = P(("dp", "seq"), None)
    tiles = P(("dp", "seq"), "chan")
    in_specs = (rows, rows, P(None, "chan"), P(), P(None, "chan"), P("chan"), P("chan"), P("chan"), tiles, tiles)
    return jax.shard_map(
        local, mesh=mesh, in_specs=in_specs, out_specs=(tiles,) * 4, check_vma=False
    )
```

time: 1060 us -> 213 us (0.20); the launches traced: 1050 us -> 211 us
  waiting for transfers between devices: 597 us -> 0 us
  other arithmetic: 132 us -> 0.7 us
  local copies, waits for them, and re-layouts: 88.7 us -> 7.73 us
  matrix products: 64.1 us -> 0 us
  blocking collectives: 147 us -> 181 us
  Pallas kernels: 0 us -> 20.4 us
  between operations: 15 us -> 0.67 us
    all_gather x4 -> x0, waiting for transfers between devices: 499 us -> none  [carried_in(): gathered = jax.tree.map(lambda a: lax.all_gather(a, axis), part)]
    all_to_all x0 -> x3, blocking collectives: none -> 181 us  [the longest x1 84.4 us: local(): arrived = lax.all_to_all(send, 'seq', 0, 0, tiled=True)]
    all_gather x2 -> x0, blocking collectives: 147 us -> none  [carried_in(): gathered = jax.tree.map(lambda a: lax.all_gather(a, axis), part)]
    add x62 -> x0, other arithmetic: 103 us -> none  [chain_combine(): latter[0][..., None, None] * earlier[1] + latter[1]]
    reduce_scatter x1 -> x0, waiting for transfers between devices: 98.5 us -> none  [local(): lax.psum_scatter(grad_term, 'chan', scatter_dimension=2, tiled=True)]
    dot_general x30 -> x0, matrix products: 64.1 us -> none  [the longest x6 18.9 us: response(): within = jnp.einsum('hts,shp->thp', weights, values, precision=highest)]
    mul x66 -> x0, local copies, waits for them, and re-layouts: 42.9 us -> none  [the longest x62 40.3 us: chain_combine(): latter[0][..., None, None] * earlier[1] + latter[1]]
    rev x12 -> x0, local copies, waits for them, and re-layouts: 24.5 us -> none  [the longest x1 7.04 us: local(): sources = jnp.stack([hidden, jnp.flip(complement, 1)])]
  transfers between devices with their start and end apart: 5 -> 0, of which waited for: 5 -> 0; matrix products, arithmetic and copies ran while one was open for 22% -> 0% of each run, Pallas kernels for 0% -> 0%
where the time goes in v1:
time: 213 us; the launch traced here: 211 us
  blocking collectives  181 us (85%)
  Pallas kernels  20.4 us (10%)
  local copies, waits for them, and re-layouts  7.73 us (4%)
    all_to_all x1, blocking collectives, local(): arrived = lax.all_to_all(send, 'seq', 0, 0, tiled=True)  84.4 us
    all_to_all x1, blocking collectives, local(): entry = lax.all_to_all(back, 'seq', 0, 0, tiled=True)  62.5 us
    all_to_all x1, blocking collectives, local(): shares = lax.all_to_all(term, 'chan', 0, 0, tiled=True)  34.4 us
    pallas_call x4, Pallas kernels, call(): pl.pallas_call(kernel, out_shape=[jax.ShapeDtypeStruct(shape, dtype) for...  20.4 us
    unnamed x15, local copies, waits for them, and re-layouts  7.73 us

profile of v1, /device:TPU:1, one launch (start us, length us, event | category | flops | bytes accessed | tf_op | source)
XLA Modules:
  0.0 210.9 jit_solution(9031631922743696585)
XLA Ops:
  0.6 1.0 copy.14.step
  1.7 0.7 select_maximum_fusion.params
  2.4 0.0 copy-start
  2.4 1.6 copy-done
  4.0 0.0 copy-start.1
  4.0 1.2 copy-done.1
  5.2 0.0 copy-start.3
  5.2 0.9 copy-done.3
  6.1 0.0 copy-start.4
  6.1 0.9 copy-done.4
  7.0 0.0 copy-start.5
  7.0 1.0 copy-done.5
  8.0 0.0 copy-start.6
  8.0 1.0 copy-done.6
  9.1 6.0 %shard_map.129 = (f32[32,136,128]{2,1,0:T(8,128)}, bf16[256,512]{1,0:T(8,128)(2,1)S(1)}, bf16[256,256]{1,0:T(8,128)(2,1)S(1)}, f32[256,128]{1,0:T(8,128)S(1)}, f32[256,128]{1,0:T(8,128)S(1)}) custom-call(bf16[128,2048]{1,0:T(8,128)(2,1)S(1)} %copy-done.5, bf16[128,2048]{1,0:T(8,128)(2,1)S(1)} %copy-done.6, bf16[2048,512]{1,0:T(8,128)(2,1)S(1)} %copy-done, ...), custom_call_target="tpu_custom_call" | custom-call | tf_op jit(solution)/shard_map/pallas_call | solution.py:295
  15.0 84.4 %all_to_all.15.arrived = f32[32,136,128]{2,1,0:T(8,128)S(1)} all-to-all(f32[32,136,128]{2,1,0:T(8,128)} %get-tuple-element.14), channel_id=1, replica_groups=mesh['seq'=32,'chan'=8,'dp'=2] {'seq'}, dimensions={0} | all-to-all | bytes 4456448 | tf_op jit(solution)/shard_map/all_to_all | solution.py:323
  99.4 0.3 shard_map.130
  99.8 0.0 copy-start.2
  99.8 62.5 %all_to_all.16.entry = f32[32,128,128]{2,1,0:T(8,128)} all-to-all(f32[32,128,128]{2,1,0:T(8,128)S(1)} %shard_map.130), channel_id=1, replica_groups=mesh['seq'=32,'chan'=8,'dp'=2] {'seq'}, dimensions={0} | all-to-all | bytes 4194304 | tf_op jit(solution)/shard_map/all_to_all | solution.py:327
  162.3 0.0 copy-done.2
  162.3 13.3 %shard_map.131 = (bf16[128,512]{1,0:T(8,128)(2,1)}, bf16[128,512]{1,0:T(8,128)(2,1)}, f32[8,256,256]{2,1,0:T(8,128)S(1)}) custom-call(f32[32,128,128]{2,1,0:T(8,128)} %all_to_all.16.entry, bf16[256,512]{1,0:T(8,128)(2,1)S(1)} %get-tuple-element.15.values, bf16[256,256]{1,0:T(8,128)(2,1)S(1)} %get-tuple-element.16.keys, ...), custom_call_target="tpu_custom_call" | custom-call | tf_op jit(solution)/shard_map/pallas_call | solution.py:295
  175.7 34.4 %all_to_all.17.shares = f32[8,256,256]{2,1,0:T(8,128)S(1)} all-to-all(f32[8,256,256]{2,1,0:T(8,128)S(1)} %get-tuple-element.21), channel_id=1, replica_groups=mesh['seq'=32,'chan'=8,'dp'=2] {'chan'}, dimensions={0} | all-to-all | bytes 4194304 | tf_op jit(solution)/shard_map/all_to_all | solution.py:343
  210.1 0.8 shard_map.132
Async XLA Ops:
  2.4 1.6 copy-start
  4.0 1.2 copy-start.1
  5.2 0.9 copy-start.3
  6.1 0.9 copy-start.4
  7.0 1.0 copy-start.5
  8.0 1.0 copy-start.6
  99.8 62.5 %copy-start.2 = (bf16[2048,256]{1,0:T(8,128)(2,1)S(1)}, bf16[2048,256]{1,0:T(8,128)(2,1)}, u32[]{:S(2)}) copy-start(bf16[2048,256]{1,0:T(8,128)(2,1)} %select.18) | copy-start | bytes 3145732

commit v2 on v1

--- a/solution.py
+++ b/solution.py
@@ -72,24 +72,64 @@
 
 
 def project_kernel(
-    hidden, complement, inner, select, step, params, cot, ccot, send, values, keys, dts, sigs, source, step_wide
+    hidden_hbm,
+    complement_hbm,
+    inner_hbm,
+    select_hbm,
+    cot_hbm,
+    ccot_hbm,
+    step,
+    params,
+    send,
+    values,
+    keys,
+    dts,
+    sigs,
+    source,
+    step_wide,
+    complement,
+    inner,
+    select,
+    cot,
+    ccot,
+    sems,
 ):
     channels = inner.shape[1]
     heads = channels // HEAD
     bias, rate = params[0:1, :], params[1:2, :]
-    depth = hidden.shape[1]
+    fetches = [
+        pltpu.make_async_copy(here, there, sems.at[i])
+        for i, (here, there) in enumerate(
+            (
+                (complement_hbm, complement),
+                (hidden_hbm, source.at[:ROWS]),
+                (select_hbm, select),
+                (inner_hbm, inner),
+                (cot_hbm, cot),
+                (ccot_hbm, ccot),
+            )
+        )
+    ]
+    for fetch in fetches:
+        fetch.start()
+    depth = complement.shape[1]
     blocks = depth // FLIP
-    source[:ROWS, :] = hidden[...]
     anti = anti_identity()
+    fetches[0].wait()
     for b in range(blocks):
         block = complement[:, (blocks - 1 - b) * FLIP : (blocks - b) * FLIP]
         source[ROWS:, b * FLIP : (b + 1) * FLIP] = dot(block, anti).astype(BF16)
+    step_wide[...] = jnp.zeros_like(step_wide)
+    step_wide[:heads, :] = step[...]
+    fetches[1].wait()
     src = source[...]
+    raw = dot(src, step_wide[...], 1, 1) + bias
+    fetches[2].wait()
+    k_all = dot(src, select[...]).astype(BF16)
+    fetches[3].wait()
     v_all = dot(src, inner[...]).astype(BF16)
-    k_all = dot(src, select[...]).astype(BF16)
-    step_wide[...] = jnp.zeros_like(step_wide)
-    step_wide[:, :heads] = step[...]
-    raw = dot(src, step_wide[...]) + bias
+    fetches[4].wait()
+    fetches[5].wait()
     small = jnp.exp(-jnp.abs(raw))
     one_more = 1.0 + small
     tail = jnp.where(
@@ -149,25 +189,20 @@
     keys,
     dts,
     sigs,
-    inner,
-    select,
-    step,
     params,
     cot,
     ccot,
     mixed,
     cmixed,
-    term,
     d_val,
-    d_key,
-    d_raw,
-    step_wide,
+    d_key_high,
+    d_key_low,
+    d_raw_high,
+    d_raw_low,
 ):
     channels = values.shape[1]
     heads = channels // HEAD
     rate, skip = params[1:2, :], params[2:3, :]
-    step_wide[...] = jnp.zeros_like(step_wide)
-    step_wide[:, :heads] = step[...]
     spread = spread_matrix(channels)
     row_id, col_id = iota((ROWS, ROWS), 0), iota((ROWS, ROWS), 1)
     diagonal, lower, upper = row_id == col_id, row_id > col_id, row_id < col_id
@@ -259,46 +294,97 @@
         from_here = where01(row_id <= col_id)
         d_log = dot(from_here, d_upto, precision=HIGHEST) + dot(where01(upper), d_before, precision=HIGHEST)
         d_log = d_log + d_total
-        d_raw[rows, :] = (d_dt - rate * d_log) * sigs[rows, :]
-        d_key[rows, :STATE] = d_write + dot_left(d_scores, read, 0, 0)
-        d_key[rows, STATE:] = d_read + dot_left(d_scores, write)
-    chunks = term.shape[0]
+        d_raw_high[rows, :], d_raw_low[rows, :] = split((d_dt - rate * d_log) * sigs[rows, :])
+        d_write = d_write + dot_left(d_scores, read, 0, 0)
+        d_read = d_read + dot_left(d_scores, write)
+        d_key_high[rows, :STATE], d_key_low[rows, :STATE] = split(d_write)
+        d_key_high[rows, STATE:], d_key_low[rows, STATE:] = split(d_read)
+
+
+def reduce_kernel(
+    ranks,
+    d_val,
+    d_key_high,
+    d_key_low,
+    d_raw_high,
+    d_raw_low,
+    inner,
+    select,
+    step,
+    first,
+    second,
+    step_wide,
+    term,
+    arrived,
+    send_sems,
+    recv_sems,
+):
+    me = lax.axis_index("chan")
     width = term.shape[2]
-    val = d_val[...]
-    key_high, key_low = split(d_key[...])
-    raw_high, raw_low = split(d_raw[...])
-    for j in range(chunks):
-        cols = slice(j * width, (j + 1) * width)
-        part = dot(val, inner[cols, :], 1, 1)
-        sel, stp = select[cols, :], step_wide[cols, :]
-        part = part + (dot(key_high, sel, 1, 1) + dot(key_low, sel, 1, 1))
-        part = part + (dot(raw_high, stp, 1, 1) + dot(raw_low, stp, 1, 1))
-        term[j, :ROWS, :] = part[:ROWS]
-        term[chunks - 1 - j, ROWS:, :] = part[ROWS:]
-
-
-def combine_kernel(shares, first, second):
-    total = shares[0]
-    for j in range(1, shares.shape[0]):
-        total = total + shares[j]
+    heads = step.shape[0]
+    barrier = pltpu.get_barrier_semaphore()
+    for j in range(1, ranks):
+        pl.semaphore_signal(
+            barrier, inc=1, device_id={"chan": lax.rem(me + j, ranks)}, device_id_type=pl.DeviceIdType.MESH
+        )
+    step_wide[...] = jnp.zeros_like(step_wide)
+    step_wide[:heads, :] = step[...]
+
+    def chunk(rows, rank):
+        at = pl.multiple_of(rank * width, width)
+        cols = pl.ds(at, width)
+        part = dot(d_val[rows, :], inner[cols, :], 1, 1)
+        keys = select[cols, :]
+        part = part + (dot(d_key_high[rows, :], keys, 1, 1) + dot(d_key_low[rows, :], keys, 1, 1))
+        steps = step_wide[:, cols]
+        return part + (dot(d_raw_high[rows, :], steps) + dot(d_raw_low[rows, :], steps))
+
+    def share(rank):
+        term[rank, :ROWS, :] = chunk(slice(0, ROWS), rank)
+        term[rank, ROWS:, :] = chunk(slice(ROWS, 2 * ROWS), ranks - 1 - rank)
+
+    def copy(j):
+        peer = lax.rem(me + j, ranks)
+        return pltpu.make_async_remote_copy(
+            src_ref=term.at[peer],
+            dst_ref=arrived.at[me],
+            send_sem=send_sems.at[j],
+            recv_sem=recv_sems.at[j],
+            device_id={"chan": peer},
+            device_id_type=pl.DeviceIdType.MESH,
+        )
+
+    share(lax.rem(me + 1, ranks))
+    pl.semaphore_wait(barrier, ranks - 1)
+    copy(1).start()
+    for j in range(2, ranks):
+        share(lax.rem(me + j, ranks))
+        copy(j).start()
+    share(me)
+    total = term[me]
+    for j in range(1, ranks):
+        copy(j).wait_recv()
+        total = total + arrived[lax.rem(me + ranks - j, ranks)]
+    for j in range(1, ranks):
+        copy(j).wait_send()
     total = total.astype(BF16)
     first[...] = total[:ROWS]
     anti = anti_identity()
-    blocks = total.shape[1] // FLIP
+    blocks = width // FLIP
     for b in range(blocks):
         block = total[ROWS:, (blocks - 1 - b) * FLIP : (blocks - b) * FLIP]
         second[:, b * FLIP : (b + 1) * FLIP] = dot(block, anti).astype(BF16)
 
 
-def call(kernel, outs, args, scratch=()):
+def call(kernel, outs, args, scratch=(), far=0, **params):
     whole = pl.BlockSpec(memory_space=pltpu.VMEM)
     return pl.pallas_call(
         kernel,
         out_shape=[jax.ShapeDtypeStruct(shape, dtype) for shape, dtype in outs],
-        in_specs=[whole] * len(args),
+        in_specs=[pl.BlockSpec(memory_space=pltpu.HBM)] * far + [whole] * (len(args) - far),
         out_specs=[whole] * len(outs),
-        scratch_shapes=[pltpu.VMEM(shape, dtype) for shape, dtype in scratch],
-        compiler_params=pltpu.CompilerParams(vmem_limit_bytes=48 << 20),
+        scratch_shapes=list(scratch),
+        compiler_params=pltpu.CompilerParams(vmem_limit_bytes=48 << 20, **params),
     )(*args)
 
 
@@ -308,6 +394,7 @@
     depth = hidden.shape[1]
     channels = heads * HEAD
     params = jnp.pad(jnp.stack([bias, rate, skip]), ((0, 5), (0, LANES - heads)))
+    step = step.T
     send, values, keys, dts, sigs = call(
         project_kernel,
         [
@@ -317,31 +404,52 @@
             ((2 * ROWS, LANES), F32),
             ((2 * ROWS, LANES), F32),
         ],
-        (hidden, complement, inner, select, step, params, cot, ccot),
-        [((2 * ROWS, depth), BF16), ((depth, LANES), BF16)],
+        (hidden, complement, inner, select, cot, ccot, step, params),
+        [
+            pltpu.VMEM((2 * ROWS, depth), BF16),
+            pltpu.VMEM((LANES, depth), BF16),
+            pltpu.VMEM((ROWS, depth), BF16),
+            pltpu.VMEM(inner.shape, BF16),
+            pltpu.VMEM(select.shape, BF16),
+            pltpu.VMEM(cot.shape, BF16),
+            pltpu.VMEM(ccot.shape, BF16),
+            pltpu.SemaphoreType.DMA((6,)),
+        ],
+        far=6,
     )
     arrived = lax.all_to_all(send, "seq", 0, 0, tiled=True)
     (back,) = call(
         functools.partial(scan_kernel, shards), [((4 * heads, 2 * HEAD, STATE), F32)], (arrived,)
     )
     entry = lax.all_to_all(back, "seq", 0, 0, tiled=True)
-    mixed, cmixed, term = call(
+    mixed, cmixed, *grads = call(
         finish_kernel,
         [
             ((ROWS, channels), BF16),
             ((ROWS, channels), BF16),
-            ((ranks, 2 * ROWS, depth // ranks), F32),
+            ((2 * ROWS, channels), BF16),
+            ((2 * ROWS, 2 * STATE), BF16),
+            ((2 * ROWS, 2 * STATE), BF16),
+            ((2 * ROWS, LANES), BF16),
+            ((2 * ROWS, LANES), BF16),
         ],
-        (entry, values, keys, dts, sigs, inner, select, step, params, cot, ccot),
+        (entry, values, keys, dts, sigs, params, cot, ccot),
+    )
+    share = (ranks, 2 * ROWS, depth // ranks)
+    first, second = call(
+        functools.partial(reduce_kernel, ranks),
+        [((ROWS, depth // ranks), BF16)] * 2,
+        (*grads, inner, select, step),
         [
-            ((2 * ROWS, channels), BF16),
-            ((2 * ROWS, 2 * STATE), F32),
-            ((2 * ROWS, LANES), F32),
-            ((depth, LANES), BF16),
+            pltpu.VMEM((LANES, depth), BF16),
+            pltpu.VMEM(share, F32),
+            pltpu.VMEM(share, F32),
+            pltpu.SemaphoreType.DMA((ranks,)),
+            pltpu.SemaphoreType.DMA((ranks,)),
         ],
-    )
-    shares = lax.all_to_all(term, "chan", 0, 0, tiled=True)
-    first, second = call(combine_kernel, [((ROWS, depth // ranks), BF16)] * 2, (shares,))
+        collective_id=1,
+        has_side_effects=True,
+    )
     return mixed, cmixed, first, second
 
 

time: 213 us -> 210 us (0.986)
  blocking collectives: 181 us -> 149 us
  Pallas kernels: 20.4 us -> 50.5 us
    all_to_all x1 -> x0, blocking collectives: 34.4 us -> none  [local(): shares = lax.all_to_all(term, 'chan', 0, 0, tiled=True)]
    pallas_call x4, Pallas kernels: 20.4 us -> 50.5 us  [call(): pl.pallas_call(kernel, out_shape=[jax.ShapeDtypeStruct(shape, dtype) for...]
    unnamed x15 -> x26, local copies, waits for them, and re-layouts: 7.73 us -> 8.75 us
where the time goes in v2:
time: 210 us
  blocking collectives  149 us (71%)
  Pallas kernels  50.5 us (24%)
  local copies, waits for them, and re-layouts  8.75 us (4%)
    all_to_all x1, blocking collectives, local(): arrived = lax.all_to_all(send, 'seq', 0, 0, tiled=True)  84.8 us
    all_to_all x1, blocking collectives, local(): entry = lax.all_to_all(back, 'seq', 0, 0, tiled=True)  64.1 us
    pallas_call x4, Pallas kernels, call(): pl.pallas_call(kernel, out_shape=[jax.ShapeDtypeStruct(shape, dtype) for...  50.5 us
    unnamed x26, local copies, waits for them, and re-layouts  8.75 us

profile of v2, /device:TPU:1, one launch (start us, length us, event | category | flops | bytes accessed | tf_op | source)
XLA Modules:
  0.0 209.7 jit_solution(8366125670729187933)
XLA Ops:
  0.6 0.7 select_maximum_fusion.params
  1.3 0.0 copy-start
  1.3 1.6 copy-done
  2.9 0.0 copy-start.2
  2.9 1.2 copy-done.2
  4.1 0.0 copy-start.4
  4.1 1.0 copy-done.4
  5.2 0.0 copy-start.5
  5.2 1.0 copy-done.5
  6.2 0.0 copy-start.6
  6.2 0.9 copy-done.6
  7.1 0.0 copy-start.8
  7.1 0.9 copy-done.8
  8.0 0.0 copy-start.10
  8.0 0.8 copy-done.10
  8.8 7.5 %shard_map.129 = (f32[32,136,128]{2,1,0:T(8,128)}, bf16[256,512]{1,0:T(8,128)(2,1)S(1)}, bf16[256,256]{1,0:T(8,128)(2,1)S(1)}, f32[256,128]{1,0:T(8,128)S(1)}, f32[256,128]{1,0:T(8,128)S(1)}) custom-call(bf16[128,2048]{1,0:T(8,128)(2,1)S(1)} %copy-done.4, bf16[128,2048]{1,0:T(8,128)(2,1)S(1)} %copy-done.5, bf16[2048,512]{1,0:T(8,128)(2,1)S(1)} %copy-done, ...), custom_call_target="tpu_custom_call" | custom-call | tf_op jit(solution)/shard_map/pallas_call | solution.py:381
  16.3 84.8 %all_to_all.10.arrived = f32[32,136,128]{2,1,0:T(8,128)S(1)} all-to-all(f32[32,136,128]{2,1,0:T(8,128)} %get-tuple-element.18), channel_id=1, replica_groups=mesh['seq'=32,'chan'=8,'dp'=2] {'seq'}, dimensions={0} | all-to-all | bytes 4456448 | tf_op jit(solution)/shard_map/all_to_all | solution.py:420
  101.1 0.3 shard_map.130
  101.5 0.0 copy-start.7
  101.5 0.0 copy-start.9
  101.5 0.0 copy-start.3
  101.5 64.1 %all_to_all.11.entry = f32[32,128,128]{2,1,0:T(8,128)S(1)} all-to-all(f32[32,128,128]{2,1,0:T(8,128)S(1)} %shard_map.130), channel_id=1, replica_groups=mesh['seq'=32,'chan'=8,'dp'=2] {'seq'}, dimensions={0} | all-to-all | bytes 4194304 | tf_op jit(solution)/shard_map/all_to_all | solution.py:424
  165.7 0.0 copy-start.1
  165.7 0.0 copy-start.11
  165.7 0.0 copy-done.7
  165.7 0.0 copy-done.9
  165.7 9.1 %shard_map.131 = (bf16[128,512]{1,0:T(8,128)(2,1)}, bf16[128,512]{1,0:T(8,128)(2,1)}, bf16[256,512]{1,0:T(8,128)(2,1)S(1)}, bf16[256,256]{1,0:T(8,128)(2,1)S(1)}...) custom-call(f32[32,128,128]{2,1,0:T(8,128)S(1)} %all_to_all.11.entry, ...), custom_call_target="tpu_custom_call" | custom-call | tf_op jit(solution)/shard_map/pallas_call | solution.py:381
  174.8 0.0 copy-done.3
  174.8 0.0 copy-done.1
  174.8 0.0 copy-done.11
  174.8 33.6 %shard_map.132 = (bf16[128,256]{1,0:T(8,128)(2,1)S(1)}, bf16[128,256]{1,0:T(8,128)(2,1)S(1)}) custom-call(bf16[256,512]{1,0:T(8,128)(2,1)S(1)} %get-tuple-element.25.d_val, bf16[256,256]{1,0:T(8,128)(2,1)S(1)} %get-tuple-element.26.d_key_high, bf16[256,256]{1,0:T(8,128)(2,1)S(1)} %get-tuple-element.27.d_key_low, ...), custom_call_target="tpu_custom_call" | custom-call | tf_op jit(solution)/shard_map/pallas_call | solution.py:381
  208.4 0.6 copy.16
  209.0 0.6 copy.17
Async XLA Ops:
  1.3 1.6 copy-start
  2.9 1.2 copy-start.2
  4.1 1.0 copy-start.4
  5.2 1.0 copy-start.5
  6.2 0.9 copy-start.6
  7.1 0.9 copy-start.8
  8.0 0.8 copy-start.10
  101.5 64.2 %copy-start.7 = (bf16[128,512]{1,0:T(8,128)(2,1)S(1)}, bf16[128,512]{1,0:T(8,128)(2,1)}, u32[]{:S(2)}) copy-start(bf16[128,512]{1,0:T(8,128)(2,1)} %cot.1) | copy-start | bytes 393220
  101.5 64.2 %copy-start.9 = (bf16[128,512]{1,0:T(8,128)(2,1)S(1)}, bf16[128,512]{1,0:T(8,128)(2,1)}, u32[]{:S(2)}) copy-start(bf16[128,512]{1,0:T(8,128)(2,1)} %ccot.1) | copy-start | bytes 393220
  101.5 73.3 %copy-start.3 = (bf16[2048,256]{1,0:T(8,128)(2,1)S(1)}, bf16[2048,256]{1,0:T(8,128)(2,1)}, u32[]{:S(2)}) copy-start(bf16[2048,256]{1,0:T(8,128)(2,1)} %select.16) | copy-start | bytes 3145732
  165.7 9.1 %copy-start.1 = (bf16[2048,512]{1,0:T(8,128)(2,1)S(1)}, bf16[2048,512]{1,0:T(8,128)(2,1)}, u32[]{:S(2)}) copy-start(bf16[2048,512]{1,0:T(8,128)(2,1)} %inner.1) | copy-start | bytes 6291460
  165.7 9.1 %copy-start.11 = (bf16[2048,8]{0,1:T(8,128)(2,1)S(1)}, bf16[2048,8]{0,1:T(8,128)(2,1)}, u32[]{:S(2)}) copy-start(bf16[2048,8]{0,1:T(8,128)(2,1)} %param.14) | copy-start | bytes 98308

commit v3 on v2

--- a/solution.py
+++ b/solution.py
@@ -15,6 +15,7 @@
 ROWS = 128
 FLIP = 256
 LANES = 128
+ROW = 4
 
 
 def dot(a, b, ca=1, cb=0, precision=None):
@@ -78,7 +79,7 @@
     select_hbm,
     cot_hbm,
     ccot_hbm,
-    step,
+    step_hbm,
     params,
     send,
     values,
@@ -92,6 +93,7 @@
     select,
     cot,
     ccot,
+    step,
     sems,
 ):
     channels = inner.shape[1]
@@ -107,6 +109,7 @@
                 (inner_hbm, inner),
                 (cot_hbm, cot),
                 (ccot_hbm, ccot),
+                (step_hbm, step),
             )
         )
     ]
@@ -120,6 +123,7 @@
         block = complement[:, (blocks - 1 - b) * FLIP : (blocks - b) * FLIP]
         source[ROWS:, b * FLIP : (b + 1) * FLIP] = dot(block, anti).astype(BF16)
     step_wide[...] = jnp.zeros_like(step_wide)
+    fetches[6].wait()
     step_wide[:heads, :] = step[...]
     fetches[1].wait()
     src = source[...]
@@ -150,48 +154,201 @@
         g = (cot if s == 0 else ccot)[...].astype(F32)
         write, read = k_all[rows, :STATE], k_all[rows, STATE:]
         widen = lambda w: dot(w, spread, precision=HIGHEST)
+        second = channels + 8 * heads
         pieces = (
             (0, 0, widen(jnp.exp(total - upto) * dt) * x, write),
-            (0, HEAD, widen(jnp.exp(total - before)) * g, read),
+            (0, second, widen(jnp.exp(total - before)) * g, read),
             (1, 0, widen(jnp.exp(before) * dt) * x, write),
-            (1, HEAD, widen(jnp.exp(upto)) * g, read),
+            (1, second, widen(jnp.exp(upto)) * g, read),
         )
         for way, at, left, right in pieces:
             state = dot_left(left, right, 0, 0)
-            first = (way * 2 + s) * heads
-            send[first : first + heads, at : at + HEAD, :] = state.reshape(heads, HEAD, STATE)
+            send[way * 2 + s, at : at + channels, :] = state
         decay = jnp.exp(dot(log_decay, ones, 0, 0, precision=HIGHEST))
         for way in range(2):
             for h in range(heads):
-                send[(way * 2 + s) * heads + h, 2 * HEAD :, :] = jnp.broadcast_to(decay[h : h + 1], (8, STATE))
-
-
-def scan_kernel(shards, arrived, back):
-    mine = arrived.shape[0] // shards
+                at = channels + 8 * h
+                send[way * 2 + s, at : at + 8, :] = jnp.broadcast_to(decay[h : h + 1], (8, STATE))
+
+
+def exchange_kernel(
+    layers,
+    heads,
+    send,
+    entry,
+    rows_in,
+    sums_a,
+    sums_b,
+    layers_a,
+    layers_b,
+    scanned_a,
+    scanned_b,
+    before_a,
+    before_b,
+    members_a,
+    members_b,
+    gather_out,
+    gather_in,
+    up_out,
+    up_in,
+    back_out,
+    back_in,
+    spread_out,
+    spread_in,
+):
     me = lax.axis_index("seq")
-    for j in range(mine):
-        down = (me * mine + j) // (shards * mine // 2)
-
-        def one(lap, state):
-            c = lap + down * (shards - 1 - 2 * lap)
-            at = c * mine + j
-            back[at] = state.reshape(2 * HEAD, STATE)
-            part = arrived[at]
-            decay = part[2 * HEAD :]
-            return state * decay[None] + part[: 2 * HEAD].reshape(2 * HEAD // 8, 8, STATE)
-
-        lax.fori_loop(0, shards, one, jnp.zeros((2 * HEAD // 8, 8, STATE), F32))
+    layer, member = me // ROW, lax.rem(me, ROW)
+    down = member // 2
+    each = heads // layers
+    channels = heads * HEAD
+    side = lambda j: layer * ROW + lax.rem(member + j, ROW)
+    over = lambda j: lax.rem(layer + j, layers) * ROW + member
+    place = {"device_id_type": pl.DeviceIdType.MESH}
+    barrier = pltpu.get_barrier_semaphore()
+    for j in range(1, ROW):
+        pl.semaphore_signal(barrier, inc=1, device_id={"seq": side(j)}, **place)
+    for j in range(1, layers):
+        pl.semaphore_signal(barrier, inc=1, device_id={"seq": over(j)}, **place)
+    pl.semaphore_wait(barrier, ROW + layers - 2)
+    spans = (pl.ds(0, channels + 8 * heads), pl.ds(channels + 8 * heads, channels))
+
+    def gather(half, j):
+        return pltpu.make_async_remote_copy(
+            src_ref=send.at[lax.rem(member + j, ROW), spans[half]],
+            dst_ref=rows_in.at[member, spans[half]],
+            send_sem=gather_out.at[half, j],
+            recv_sem=gather_in.at[half, j],
+            device_id={"seq": side(j)},
+            **place,
+        )
+
+    def up(half, j):
+        sums, layered = ((sums_a, layers_a), (sums_b, layers_b))[half]
+        return pltpu.make_async_remote_copy(
+            src_ref=sums.at[lax.rem(layer + j, layers)],
+            dst_ref=layered.at[layer],
+            send_sem=up_out.at[half, j],
+            recv_sem=up_in.at[half, j],
+            device_id={"seq": over(j)},
+            **place,
+        )
+
+    def give_back(half, j):
+        scanned, before = ((scanned_a, before_a), (scanned_b, before_b))[half]
+        return pltpu.make_async_remote_copy(
+            src_ref=scanned.at[lax.rem(layer + j, layers)],
+            dst_ref=before.at[layer],
+            send_sem=back_out.at[half, j],
+            recv_sem=back_in.at[half, j],
+            device_id={"seq": over(j)},
+            **place,
+        )
+
+    def spread(half, j):
+        members = (members_a, members_b)[half]
+        return pltpu.make_async_remote_copy(
+            src_ref=members.at[lax.rem(member + j, ROW)],
+            dst_ref=entry.at[member, half],
+            send_sem=spread_out.at[half, j],
+            recv_sem=spread_in.at[half, j],
+            device_id={"seq": side(j)},
+            **place,
+        )
+
+    order = (1, 3, 2)
+    far = tuple(j for j in (1, 7, 2, 6, 3, 5, 4) if j < layers)
+    for half in range(2):
+        for j in order:
+            gather(half, j).start()
+    rows_in[member] = send[member]
+    zero = jnp.zeros((HEAD // 8, 8, STATE), F32)
+
+    def part(source, h, half):
+        at = h * HEAD + half * (channels + 8 * heads)
+        return rows_in[source, pl.ds(pl.multiple_of(at, 8), HEAD), :].reshape(HEAD // 8, 8, STATE)
+
+    def decay(source, h):
+        return rows_in[source, pl.ds(pl.multiple_of(channels + 8 * h, 8), 8), :]
+
+    def turned(lap, count):
+        return lap + down * (count - 1 - 2 * lap)
+
+    for half in range(2):
+        sums, layered, scanned, before, members = (
+            (sums_a, layers_a, scanned_a, before_a, members_a),
+            (sums_b, layers_b, scanned_b, before_b, members_b),
+        )[half]
+        for j in order:
+            gather(half, j).wait_recv()
+
+        def total(h, carry):
+            state = zero
+            through = jnp.ones((8, STATE), F32)
+            for m in range(ROW):
+                source = turned(m, ROW)
+                step = decay(source, h)
+                state = state * step[None] + part(source, h, half)
+                through = through * step
+            sums[h // each, h % each, :HEAD, :] = state.reshape(HEAD, STATE)
+            if half == 0:
+                sums[h // each, h % each, HEAD:, :] = through
+            return carry
+
+        lax.fori_loop(0, heads, total, 0)
+        for j in far:
+            up(half, j).start()
+        layered[layer] = sums[layer]
+        for j in far:
+            up(half, j).wait_recv()
+        for e in range(each):
+
+            def scan(lap, state):
+                at = turned(lap, layers)
+                scanned[at, e] = state.reshape(HEAD, STATE)
+                step = layers_a[at, e, HEAD:, :]
+                return state * step[None] + layered[at, e, :HEAD, :].reshape(HEAD // 8, 8, STATE)
+
+            lax.fori_loop(0, layers, scan, zero)
+        for j in far:
+            give_back(half, j).start()
+        before[layer] = scanned[layer]
+        for j in far:
+            give_back(half, j).wait_recv()
+
+        def unfold(h, carry):
+            state = before[h // each, h % each].reshape(HEAD // 8, 8, STATE)
+            for m in range(ROW):
+                target = turned(m, ROW)
+                members[target, pl.ds(pl.multiple_of(h * HEAD, 8), HEAD), :] = state.reshape(HEAD, STATE)
+                if m < ROW - 1:
+                    state = state * decay(target, h)[None] + part(target, h, half)
+            return carry
+
+        lax.fori_loop(0, heads, unfold, 0)
+        for j in order:
+            spread(half, j).start()
+        entry[member, half] = members[member]
+    for half in range(2):
+        for j in order:
+            spread(half, j).wait_recv()
+    for half in range(2):
+        for j in order:
+            gather(half, j).wait_send()
+            spread(half, j).wait_send()
+        for j in far:
+            up(half, j).wait_send()
+            give_back(half, j).wait_send()
 
 
 def finish_kernel(
+    cot_hbm,
+    ccot_hbm,
     entry,
     values,
     keys,
     dts,
     sigs,
     params,
-    cot,
-    ccot,
     mixed,
     cmixed,
     d_val,
@@ -199,7 +356,16 @@
     d_key_low,
     d_raw_high,
     d_raw_low,
+    cot,
+    ccot,
+    sems,
 ):
+    fetches = [
+        pltpu.make_async_copy(cot_hbm, cot, sems.at[0]),
+        pltpu.make_async_copy(ccot_hbm, ccot, sems.at[1]),
+    ]
+    for fetch in fetches:
+        fetch.start()
     channels = values.shape[1]
     heads = channels // HEAD
     rate, skip = params[1:2, :], params[2:3, :]
@@ -222,16 +388,14 @@
         dt_t = dot(dt, eye, 0, 0, precision=HIGHEST)
         before_t = dot(log_decay, where01(upper), 0, 0, precision=HIGHEST)
         upto_t = before_t + dot(log_decay, eye, 0, 0, precision=HIGHEST)
+        fetches[s].wait()
         x_b, g_b = values[rows, :], (cot if s == 0 else ccot)[...]
         x, g = x_b.astype(F32), g_b.astype(F32)
         write, read = keys[rows, :STATE], keys[rows, STATE:]
         u_fwd, u_bwd = widen(jnp.exp(total - upto)), widen(jnp.exp(before))
         w_fwd, w_bwd = widen(jnp.exp(upto)), widen(jnp.exp(total - before))
         dt_wide = widen(dt)
-        state = lambda way, at: entry[
-            (way * 2 + s) * heads : (way * 2 + s + 1) * heads, at : at + HEAD, :
-        ].reshape(heads * HEAD, STATE)
-        h_in, m_in, k_in, l_in = state(0, 0), state(0, HEAD), state(1, 0), state(1, HEAD)
+        h_in, m_in, k_in, l_in = entry[s, 0], entry[s, 1], entry[2 + s, 0], entry[2 + s, 1]
         y_fwd = w_fwd * dot_right(read, h_in, 1, 1)
         y_bwd = w_bwd * dot_right(read, k_in, 1, 1)
         x_l = u_fwd * dot_right(write, l_in, 1, 1)
@@ -303,22 +467,33 @@
 
 def reduce_kernel(
     ranks,
+    inner_hbm,
+    select_hbm,
+    step_hbm,
     d_val,
     d_key_high,
     d_key_low,
     d_raw_high,
     d_raw_low,
+    first,
+    second,
     inner,
     select,
     step,
-    first,
-    second,
     step_wide,
     term,
     arrived,
+    sems,
     send_sems,
     recv_sems,
 ):
+    fetches = [
+        pltpu.make_async_copy(inner_hbm, inner, sems.at[0]),
+        pltpu.make_async_copy(select_hbm, select, sems.at[1]),
+        pltpu.make_async_copy(step_hbm, step, sems.at[2]),
+    ]
+    for fetch in fetches:
+        fetch.start()
     me = lax.axis_index("chan")
     width = term.shape[2]
     heads = step.shape[0]
@@ -328,6 +503,8 @@
             barrier, inc=1, device_id={"chan": lax.rem(me + j, ranks)}, device_id_type=pl.DeviceIdType.MESH
         )
     step_wide[...] = jnp.zeros_like(step_wide)
+    for fetch in fetches:
+        fetch.wait()
     step_wide[:heads, :] = step[...]
 
     def chunk(rows, rank):
@@ -385,7 +562,7 @@
         out_specs=[whole] * len(outs),
         scratch_shapes=list(scratch),
         compiler_params=pltpu.CompilerParams(vmem_limit_bytes=48 << 20, **params),
-    )(*args)
+    )(*[pltpu.with_memory_space_constraint(a, pltpu.HBM) for a in args[:far]], *args[far:])
 
 
 def local(hidden, complement, inner, select, step, bias, rate, skip, cot, ccot):
@@ -398,7 +575,7 @@
     send, values, keys, dts, sigs = call(
         project_kernel,
         [
-            ((4 * heads, 2 * HEAD + 8, STATE), F32),
+            ((4, 2 * channels + 8 * heads, STATE), F32),
             ((2 * ROWS, channels), BF16),
             ((2 * ROWS, 2 * STATE), BF16),
             ((2 * ROWS, LANES), F32),
@@ -413,15 +590,43 @@
             pltpu.VMEM(select.shape, BF16),
             pltpu.VMEM(cot.shape, BF16),
             pltpu.VMEM(ccot.shape, BF16),
-            pltpu.SemaphoreType.DMA((6,)),
+            pltpu.VMEM(step.shape, BF16),
+            pltpu.SemaphoreType.DMA((7,)),
         ],
-        far=6,
+        far=7,
     )
-    arrived = lax.all_to_all(send, "seq", 0, 0, tiled=True)
-    (back,) = call(
-        functools.partial(scan_kernel, shards), [((4 * heads, 2 * HEAD, STATE), F32)], (arrived,)
+    layers = shards // ROW
+    each = heads // layers
+    halves = lambda rows: pltpu.VMEM((layers, each, rows, STATE), F32)
+    dma = lambda count: pltpu.SemaphoreType.DMA((2, count))
+    (entry,) = call(
+        functools.partial(exchange_kernel, layers, heads),
+        [((4, 2, channels, STATE), F32)],
+        (send,),
+        [
+            pltpu.VMEM(send.shape, F32),
+            halves(HEAD + 8),
+            halves(HEAD),
+            halves(HEAD + 8),
+            halves(HEAD),
+            halves(HEAD),
+            halves(HEAD),
+            halves(HEAD),
+            halves(HEAD),
+            pltpu.VMEM((ROW, channels, STATE), F32),
+            pltpu.VMEM((ROW, channels, STATE), F32),
+            dma(ROW),
+            dma(ROW),
+            dma(layers),
+            dma(layers),
+            dma(layers),
+            dma(layers),
+            dma(ROW),
+            dma(ROW),
+        ],
+        collective_id=2,
+        has_side_effects=True,
     )
-    entry = lax.all_to_all(back, "seq", 0, 0, tiled=True)
     mixed, cmixed, *grads = call(
         finish_kernel,
         [
@@ -433,20 +638,27 @@
             ((2 * ROWS, LANES), BF16),
             ((2 * ROWS, LANES), BF16),
         ],
-        (entry, values, keys, dts, sigs, params, cot, ccot),
+        (cot, ccot, entry, values, keys, dts, sigs, params),
+        [pltpu.VMEM(cot.shape, BF16), pltpu.VMEM(ccot.shape, BF16), pltpu.SemaphoreType.DMA((2,))],
+        far=2,
     )
     share = (ranks, 2 * ROWS, depth // ranks)
     first, second = call(
         functools.partial(reduce_kernel, ranks),
         [((ROWS, depth // ranks), BF16)] * 2,
-        (*grads, inner, select, step),
+        (inner, select, step, *grads),
         [
+            pltpu.VMEM(inner.shape, BF16),
+            pltpu.VMEM(select.shape, BF16),
+            pltpu.VMEM(step.shape, BF16),
             pltpu.VMEM((LANES, depth), BF16),
             pltpu.VMEM(share, F32),
             pltpu.VMEM(share, F32),
+            pltpu.SemaphoreType.DMA((3,)),
             pltpu.SemaphoreType.DMA((ranks,)),
             pltpu.SemaphoreType.DMA((ranks,)),
         ],
+        far=3,
         collective_id=1,
         has_side_effects=True,
     )

time: 210 us -> 161 us (0.77)
  the two profiles are of different devices: /device:TPU:1 before, /device:TPU:64 now
where the time goes in v3:
time: 161 us
  Pallas kernels  158 us (98%)
    pallas_call x4, Pallas kernels, call(): pl.pallas_call(kernel, out_shape=[jax.ShapeDtypeStruct(shape, dtype) for...  158 us

profile of v3, /device:TPU:64, one launch (start us, length us, event | category | flops | bytes accessed | tf_op | source)
XLA Modules:
  0.0 160.6 jit_solution(11495170123942327572)
XLA Ops:
  0.6 0.7 select_maximum_fusion.params
  1.3 7.3 %shard_map.129 = (f32[4,1088,128]{2,1,0:T(8,128)S(1)}, bf16[256,512]{1,0:T(8,128)(2,1)S(1)}, bf16[256,256]{1,0:T(8,128)(2,1)S(1)}, f32[256,128]{1,0:T(8,128)S(1)}, f32[256,128]{1,0:T(8,128)S(1)}) custom-call(bf16[128,2048]{1,0:T(8,128)(2,1)} %hidden_hbm.1, bf16[128,2048]{1,0:T(8,128)(2,1)} %complement_hbm.1, bf16[2048,512]{1,0:T(8,128)(2,1)} %inner_hbm.3, ...), custom_call_target="tpu_custom_call" | custom-call | tf_op jit(solution)/shard_map/pallas_call | solution.py:558
  8.6 118.5 %shard_map.130.entry = f32[4,2,512,128]{3,2,1,0:T(8,128)S(1)} custom-call(f32[4,1088,128]{2,1,0:T(8,128)S(1)} %get-tuple-element.18.send), custom_call_target="tpu_custom_call" | custom-call | tf_op jit(solution)/shard_map/pallas_call | solution.py:558
  127.2 10.1 %shard_map.131 = (bf16[128,512]{1,0:T(8,128)(2,1)}, bf16[128,512]{1,0:T(8,128)(2,1)}, bf16[256,512]{1,0:T(8,128)(2,1)S(1)}, bf16[256,256]{1,0:T(8,128)(2,1)S(1)}...) custom-call(bf16[128,512]{1,0:T(8,128)(2,1)} %cot_hbm.3, ...), custom_call_target="tpu_custom_call" | custom-call | tf_op jit(solution)/shard_map/pallas_call | solution.py:558
  137.3 22.1 %shard_map.132 = (bf16[128,256]{1,0:T(8,128)(2,1)S(1)}, bf16[128,256]{1,0:T(8,128)(2,1)S(1)}) custom-call(bf16[2048,512]{1,0:T(8,128)(2,1)} %inner_hbm.3, bf16[2048,256]{1,0:T(8,128)(2,1)} %select_hbm.3, bf16[8,2048]{1,0:T(8,128)(2,1)} %bitcast.5, bf16[256,512]{1,0:T(8,128)(2,1)S(1)} %get-tuple-element.25.d_val, ...), custom_call_target="tpu_custom_call" | custom-call | tf_op jit(solution)/shard_map/pallas_call | solution.py:558
  159.4 0.6 copy.16
  160.0 0.6 copy.17

commit v4 on v2

v4 whole, which is shorter than its diff:
```python
import functools

import jax
import jax.numpy as jnp
from jax import lax
from jax.experimental import pallas as pl
from jax.experimental.pallas import tpu as pltpu
from jax.sharding import PartitionSpec as P

F32 = jnp.float32
BF16 = jnp.bfloat16
HIGHEST = lax.Precision.HIGHEST
HEAD = 64
STATE = 128
ROWS = 128
FLIP = 256
LANES = 128
ROW = 4


def dot(a, b, ca=1, cb=0, precision=None):
    return lax.dot_general(
        a, b, (((ca,), (cb,)), ((), ())), precision=precision, preferred_element_type=F32
    )


def split(a):
    high = a.astype(BF16)
    return high, (a - high.astype(F32)).astype(BF16)


def dot_left(a, b, ca=1, cb=0):
    high, low = split(a)
    return dot(high, b, ca, cb) + dot(low, b, ca, cb)


def dot_right(a, b, ca=1, cb=0):
    high, low = split(b)
    return dot(a, high, ca, cb) + dot(a, low, ca, cb)


def dot_both(a, b, ca=1, cb=0):
    a_high, a_low = split(a)
    b_high, b_low = split(b)
    return dot(a_high, b_high, ca, cb) + (dot(a_high, b_low, ca, cb) + dot(a_low, b_high, ca, cb))


def iota(shape, dim):
    return lax.broadcasted_iota(jnp.int32, shape, dim)


def where01(mask, dtype=F32):
    return jnp.where(mask, 1.0, 0.0).astype(dtype)


def anti_identity():
    return where01(iota((FLIP, FLIP), 0) + iota((FLIP, FLIP), 1) == FLIP - 1, BF16)


def spread_matrix(channels):
    lanes = iota((LANES, channels), 1)
    row = iota((LANES, channels), 0) * HEAD
    return where01((lanes >= row) & (lanes < row + HEAD), BF16)


def decay_parts(dt, rate):
    log_decay = -dt * rate
    strict = where01(iota((ROWS, ROWS), 0) > iota((ROWS, ROWS), 1))
    before = dot(strict, log_decay, precision=HIGHEST)
    upto = before + log_decay
    total = upto[ROWS - 1 : ROWS, :]
    return log_decay, before, upto, total


def project_kernel(
    hidden_hbm,
    complement_hbm,
    inner_hbm,
    select_hbm,
    cot_hbm,
    ccot_hbm,
    step_hbm,
    params,
    send,
    values,
    keys,
    dts,
    sigs,
    source,
    step_wide,
    complement,
    inner,
    select,
    cot,
    ccot,
    step,
    sems,
):
    channels = inner.shape[1]
    heads = channels // HEAD
    bias, rate = params[0:1, :], params[1:2, :]
    fetches = [
        pltpu.make_async_copy(here, there, sems.at[i])
        for i, (here, there) in enumerate(
            (
                (complement_hbm, complement),
                (hidden_hbm, source.at[:ROWS]),
                (select_hbm, select),
                (inner_hbm, inner),
                (cot_hbm, cot),
                (ccot_hbm, ccot),
                (step_hbm, step),
            )
        )
    ]
    for fetch in fetches:
        fetch.start()
    depth = complement.shape[1]
    blocks = depth // FLIP
    anti = anti_identity()
    fetches[0].wait()
    for b in range(blocks):
        block = complement[:, (blocks - 1 - b) * FLIP : (blocks - b) * FLIP]
        source[ROWS:, b * FLIP : (b + 1) * FLIP] = dot(block, anti).astype(BF16)
    step_wide[...] = jnp.zeros_like(step_wide)
    fetches[6].wait()
    step_wide[:heads, :] = step[...]
    fetches[1].wait()
    src = source[...]
    raw = dot(src, step_wide[...], 1, 1) + bias
    fetches[2].wait()
    k_all = dot(src, select[...]).astype(BF16)
    fetches[3].wait()
    v_all = dot(src, inner[...]).astype(BF16)
    fetches[4].wait()
    fetches[5].wait()
    small = jnp.exp(-jnp.abs(raw))
    one_more = 1.0 + small
    tail = jnp.where(
        one_more == 1.0, small, jnp.log(one_more) * (small / jnp.where(one_more == 1.0, 1.0, one_more - 1.0))
    )
    dt_all = jnp.maximum(raw, 0.0) + tail
    values[...] = v_all
    keys[...] = k_all
    dts[...] = dt_all
    sigs[...] = jnp.where(raw >= 0.0, 1.0, small) / one_more
    spread = spread_matrix(channels)
    ones = jnp.ones((ROWS, STATE), F32)
    for s in range(2):
        rows = slice(s * ROWS, (s + 1) * ROWS)
        dt = dt_all[rows]
        log_decay, before, upto, total = decay_parts(dt, rate)
        x = v_all[rows].astype(F32)
        g = (cot if s == 0 else ccot)[...].astype(F32)
        write, read = k_all[rows, :STATE], k_all[rows, STATE:]
        widen = lambda w: dot_left(w, spread)
        pieces = (
            (0, 0, widen(jnp.exp(total - upto) * dt) * x, write),
            (0, 1, widen(jnp.exp(total - before)) * g, read),
            (1, 0, widen(jnp.exp(before) * dt) * x, write),
            (1, 1, widen(jnp.exp(upto)) * g, read),
        )
        for way, kind, left, right in pieces:
            state = dot_left(left, right, 0, 0)
            send[way * 2 + kind, s, :channels, :] = state
        decay = jnp.exp(dot(log_decay, ones, 0, 0, precision=HIGHEST))
        for q in range(ROW):
            for h in range(heads):
                at = channels + 8 * h
                send[q, s, at : at + 8, :] = jnp.broadcast_to(decay[h : h + 1], (8, STATE))


def within_chunk(s, values, keys, dts, rate, g_b, y_in, d_in, key_in, row_sums, column_sums):
    heads = values.shape[1] // HEAD
    row_id, col_id = iota((ROWS, ROWS), 0), iota((ROWS, ROWS), 1)
    diagonal, lower, upper = row_id == col_id, row_id > col_id, row_id < col_id
    eye = where01(diagonal)
    twice = jnp.where(diagonal, 2.0, 1.0)
    lane_first = where01(iota((1, 2 * HEAD), 1) < HEAD, BF16)
    lane_second = where01(iota((1, 2 * HEAD), 1) >= HEAD, BF16)
    head_lane = iota((ROWS, LANES), 1)
    rows = slice(s * ROWS, (s + 1) * ROWS)
    dt = dts[rows, :]
    log_decay, before, upto, total = decay_parts(dt, rate)
    dt_t = dot(dt, eye, 0, 0, precision=HIGHEST)
    before_t = dot(log_decay, where01(upper), 0, 0, precision=HIGHEST)
    upto_t = before_t + dot(log_decay, eye, 0, 0, precision=HIGHEST)
    write, read = keys[rows, :STATE], keys[rows, STATE:]
    scores = dot(read, write, 1, 1)
    d_scores = jnp.zeros((ROWS, ROWS), F32)
    by_row = jnp.zeros((ROWS, LANES), F32)
    by_row_up = jnp.zeros((ROWS, LANES), F32)
    for pair in range(heads // 2):
        lanes = slice(pair * 2 * HEAD, (pair + 1) * 2 * HEAD)
        x_pair, g_pair = values[rows, lanes], g_b[:, lanes]
        y_pair = jnp.zeros((ROWS, 2 * HEAD), F32)
        d_pair = jnp.zeros((ROWS, 2 * HEAD), F32)
        for half, lane_mask in ((0, lane_first), (1, lane_second)):
            h = pair * 2 + half
            x_h, g_h = x_pair * lane_mask, g_pair * lane_mask
            gap = jnp.where(
                upper,
                before_t[h : h + 1, :] - before[:, h : h + 1],
                upto[:, h : h + 1] - upto_t[h : h + 1, :],
            )
            decay = jnp.exp(jnp.minimum(gap, 0.0)) * twice
            dt_row = dt_t[h : h + 1, :]
            scaled = scores * decay
            w_high, w_low = split(scaled * dt_row)
            y_pair = y_pair + (dot(w_high, x_h) + dot(w_low, x_h))
            d_pair = d_pair + (dot(w_high, g_h, 0, 0) + dot(w_low, g_h, 0, 0))
            outer = dot(g_h, x_pair, 1, 1)
            grads = outer * scaled
            d_scores = d_scores + outer * (decay * dt_row)
            q = grads * dt_row
            q_low, q_up = jnp.where(lower, q, 0.0), jnp.where(upper, q, 0.0)
            by_row = jnp.where(head_lane == h, jnp.sum(q_low, 1, keepdims=True), by_row)
            by_row_up = jnp.where(head_lane == h, jnp.sum(q_up, 1, keepdims=True), by_row_up)
            column_sums[s, h : h + 1, :] = jnp.sum(grads, 0, keepdims=True)
            column_sums[s, heads + h : heads + h + 1, :] = jnp.sum(q_low, 0, keepdims=True)
            column_sums[s, 2 * heads + h : 2 * heads + h + 1, :] = jnp.sum(q_up, 0, keepdims=True)
        y_in[rows, lanes] = y_pair
        d_in[rows, lanes] = d_pair
    row_sums[s, 0] = by_row
    row_sums[s, 1] = by_row_up
    key_in[rows, :STATE] = dot_left(d_scores, read, 0, 0)
    key_in[rows, STATE:] = dot_left(d_scores, write)


def finish(
    s,
    entry,
    values,
    keys,
    dts,
    sigs,
    params,
    g_b,
    y_in,
    d_in,
    key_in,
    row_sums,
    column_sums,
    mixed,
    d_val,
    d_key_high,
    d_key_low,
    d_raw_high,
    d_raw_low,
):
    channels = values.shape[1]
    heads = channels // HEAD
    rate, skip = params[1:2, :], params[2:3, :]
    spread = spread_matrix(channels)
    row_id, col_id = iota((ROWS, ROWS), 0), iota((ROWS, ROWS), 1)
    widen = lambda w: dot_left(w, spread)
    narrow = lambda w: dot_left(w, spread, 1, 1)
    skip_wide = widen(skip)
    rows = slice(s * ROWS, (s + 1) * ROWS)
    dt = dts[rows, :]
    log_decay, before, upto, total = decay_parts(dt, rate)
    x, g = values[rows, :].astype(F32), g_b.astype(F32)
    write, read = keys[rows, :STATE], keys[rows, STATE:]
    u_fwd, u_bwd = widen(jnp.exp(total - upto)), widen(jnp.exp(before))
    w_fwd, w_bwd = widen(jnp.exp(upto)), widen(jnp.exp(total - before))
    dt_wide = widen(dt)
    h_in, m_in, k_in, l_in = entry[0, s], entry[1, s], entry[2, s], entry[3, s]
    y_fwd = w_fwd * dot_right(read, h_in, 1, 1)
    y_bwd = w_bwd * dot_right(read, k_in, 1, 1)
    x_l = u_fwd * dot_right(write, l_in, 1, 1)
    x_m = u_bwd * dot_right(write, m_in, 1, 1)
    d_read = dot_both(w_fwd * g, h_in) + dot_both(w_bwd * g, k_in)
    d_write = dot_both(u_fwd * dt_wide * x, l_in) + dot_both(u_bwd * dt_wide * x, m_in)
    r_fwd, r_bwd = narrow(g * y_fwd), narrow(g * y_bwd)
    q_fwd, q_bwd = narrow(x * x_l), narrow(x * x_m)
    both = dot_right(spread, l_in * h_in + m_in * k_in)
    both = dot(jnp.ones((8, STATE), F32), both, 1, 1, precision=HIGHEST)[0:1]
    out = y_in[rows, :] + y_fwd + y_bwd + skip_wide * x
    mixed[...] = out.astype(BF16)
    d_val[rows, :] = (d_in[rows, :] + dt_wide * (x_l + x_m) + skip_wide * g).astype(BF16)
    sums = column_sums[s]
    picked = lambda at: dot_left(sums, where01((row_id == col_id + at) & (col_id < heads), BF16), 0, 0)
    d_dt = picked(0) + q_fwd + q_bwd
    d_upto = row_sums[s, 0] - picked(heads) + r_fwd - dt * q_fwd
    d_before = picked(2 * heads) - row_sums[s, 1] - r_bwd + dt * q_bwd
    d_total = jnp.sum(r_bwd + dt * q_fwd, 0, keepdims=True) + jnp.exp(total) * both
    d_log = dot(where01(row_id <= col_id), d_upto, precision=HIGHEST)
    d_log = d_log + dot(where01(row_id < col_id), d_before, precision=HIGHEST) + d_total
    d_raw_high[rows, :], d_raw_low[rows, :] = split((d_dt - rate * d_log) * sigs[rows, :])
    d_key_high[rows, :STATE], d_key_low[rows, :STATE] = split(d_write + key_in[rows, :STATE])
    d_key_high[rows, STATE:], d_key_low[rows, STATE:] = split(d_read + key_in[rows, STATE:])


def main_kernel(
    layers,
    ranks,
    cot_hbm,
    ccot_hbm,
    inner_hbm,
    select_hbm,
    step_hbm,
    send,
    values,
    keys,
    dts,
    sigs,
    params,
    mixed,
    cmixed,
    first,
    second,
    cot,
    ccot,
    inner,
    select,
    step,
    step_wide,
    entry,
    y_in,
    d_in,
    key_in,
    row_sums,
    column_sums,
    d_val,
    d_key_high,
    d_key_low,
    d_raw_high,
    d_raw_low,
    rows_in,
    sums,
    layered,
    scanned,
    before,
    members,
    term,
    shares,
    sems,
    gather_out,
    gather_in,
    up_out,
    up_in,
    back_out,
    back_in,
    spread_out,
    spread_in,
    share_out,
    share_in,
):
    fetches = [
        pltpu.make_async_copy(here, there, sems.at[i])
        for i, (here, there) in enumerate(
            ((cot_hbm, cot), (ccot_hbm, ccot), (inner_hbm, inner), (select_hbm, select), (step_hbm, step))
        )
    ]
    for fetch in fetches:
        fetch.start()
    me, rank = lax.axis_index("seq"), lax.axis_index("chan")
    channels = values.shape[1]
    heads = channels // HEAD
    width = term.shape[3]
    layer, member = me // ROW, lax.rem(me, ROW)
    down = member // 2
    each = heads // layers
    side = lambda j: layer * ROW + lax.rem(member + j, ROW)
    over = lambda j: lax.rem(layer + j, layers) * ROW + member
    across = lambda j: lax.rem(rank + j, ranks)
    place = {"device_id_type": pl.DeviceIdType.MESH}
    barrier = pltpu.get_barrier_semaphore()
    for j in range(1, ROW):
        pl.semaphore_signal(barrier, inc=1, device_id={"seq": side(j)}, **place)
    for j in range(1, layers):
        pl.semaphore_signal(barrier, inc=1, device_id={"seq": over(j)}, **place)
    for j in range(1, ranks):
        pl.semaphore_signal(barrier, inc=1, device_id={"chan": across(j)}, **place)
    pl.semaphore_wait(barrier, ROW + layers + ranks - 3)

    def copy(here, there, sent, got, device):
        return pltpu.make_async_remote_copy(
            src_ref=here, dst_ref=there, send_sem=sent, recv_sem=got, device_id=device, **place
        )

    def gather(half, j):
        peer = lax.rem(member + j, ROW)
        there = rows_in.at[member, half]
        return copy(send.at[peer, half], there, gather_out.at[half, j], gather_in.at[half, j], {"seq": side(j)})

    def up(half, j):
        peer = lax.rem(layer + j, layers)
        there = layered.at[half, layer]
        return copy(sums.at[half, peer], there, up_out.at[half, j], up_in.at[half, j], {"seq": over(j)})

    def give_back(half, j):
        peer = lax.rem(layer + j, layers)
        there = before.at[half, layer]
        return copy(scanned.at[half, peer], there, back_out.at[half, j], back_in.at[half, j], {"seq": over(j)})

    def spread(half, j):
        peer = lax.rem(member + j, ROW)
        there = entry.at[member, half]
        return copy(members.at[half, peer], there, spread_out.at[half, j], spread_in.at[half, j], {"seq": side(j)})

    def share(half, j):
        there = shares.at[half, rank]
        return copy(term.at[half, across(j)], there, share_out.at[half, j], share_in.at[half, j], {"chan": across(j)})

    order = (1, 3, 2)
    far = tuple(j for j in (1, 7, 2, 6, 3, 5, 4) if j < layers)
    for half in range(2):
        for j in order:
            gather(half, j).start()
    rows_in[member] = send[member]
    column_sums[...] = jnp.zeros_like(column_sums)
    step_wide[...] = jnp.zeros_like(step_wide)
    for s, g in ((0, cot), (1, ccot)):
        fetches[s].wait()
        within_chunk(s, values, keys, dts, params[1:2, :], g[...], y_in, d_in, key_in, row_sums, column_sums)
    for fetch in fetches[2:]:
        fetch.wait()
    step_wide[:heads, :] = step[...]
    zero = jnp.zeros((HEAD // 8, 8, STATE), F32)

    def part(source, h, half):
        return rows_in[source, half, pl.ds(pl.multiple_of(h * HEAD, 8), HEAD), :].reshape(HEAD // 8, 8, STATE)

    def decay(source, h, half):
        return rows_in[source, half, pl.ds(pl.multiple_of(channels + 8 * h, 8), 8), :]

    def turned(lap, count):
        return lap + down * (count - 1 - 2 * lap)

    for half in range(2):
        for j in order:
            gather(half, j).wait_recv()

        def total(h, carry):
            state = zero
            through = jnp.ones((8, STATE), F32)
            for m in range(ROW):
                source = turned(m, ROW)
                slower = decay(source, h, half)
                state = state * slower[None] + part(source, h, half)
                through = through * slower
            sums[half, h // each, h % each, :HEAD, :] = state.reshape(HEAD, STATE)
            sums[half, h // each, h % each, HEAD:, :] = through
            return carry

        lax.fori_loop(0, heads, total, 0)
        for j in far:
            up(half, j).start()
        layered[half, layer] = sums[half, layer]
        for j in far:
            up(half, j).wait_recv()
        for e in range(each):

            def scan(lap, state):
                at = turned(lap, layers)
                scanned[half, at, e] = state.reshape(HEAD, STATE)
                slower = layered[half, at, e, HEAD:, :]
                return state * slower[None] + layered[half, at, e, :HEAD, :].reshape(HEAD // 8, 8, STATE)

            lax.fori_loop(0, layers, scan, zero)
        for j in far:
            give_back(half, j).start()
        before[half, layer] = scanned[half, layer]
        for j in far:
            give_back(half, j).wait_recv()

        def unfold(h, carry):
            state = before[half, h // each, h % each].reshape(HEAD // 8, 8, STATE)
            for m in range(ROW):
                target = turned(m, ROW)
                members[half, target, pl.ds(pl.multiple_of(h * HEAD, 8), HEAD), :] = state.reshape(HEAD, STATE)
                if m < ROW - 1:
                    state = state * decay(target, h, half)[None] + part(target, h, half)
            return carry

        lax.fori_loop(0, heads, unfold, 0)
        for j in order:
            spread(half, j).start()
        entry[member, half] = members[half, member]

    def chunk(half, block):
        rows = slice(half * ROWS, (half + 1) * ROWS)
        cols = pl.ds(pl.multiple_of(block * width, width), width)
        value = dot(d_val[rows, :], inner[cols, :], 1, 1)
        picked = select[cols, :]
        value = value + (dot(d_key_high[rows, :], picked, 1, 1) + dot(d_key_low[rows, :], picked, 1, 1))
        steps = step_wide[:, cols]
        return value + (dot(d_raw_high[rows, :], steps) + dot(d_raw_low[rows, :], steps))

    for s, g, out in ((0, cot, mixed), (1, ccot, cmixed)):
        for j in order:
            spread(s, j).wait_recv()
        finish(
            s,
            entry,
            values,
            keys,
            dts,
            sigs,
            params,
            g[...],
            y_in,
            d_in,
            key_in,
            row_sums,
            column_sums,
            out,
            d_val,
            d_key_high,
            d_key_low,
            d_raw_high,
            d_raw_low,
        )
        for j in range(1, ranks + 1):
            peer = across(j)
            term[s, peer] = chunk(s, ranks - 1 - peer if s else peer)
            if j < ranks:
                share(s, j).start()
    anti = anti_identity()
    for s in range(2):
        result = term[s, rank]
        for j in range(1, ranks):
            share(s, j).wait_recv()
            result = result + shares[s, across(ranks - j)]
        result = result.astype(BF16)
        if s == 0:
            first[...] = result
        else:
            blocks = width // FLIP
            for b in range(blocks):
                block = result[:, (blocks - 1 - b) * FLIP : (blocks - b) * FLIP]
                second[:, b * FLIP : (b + 1) * FLIP] = dot(block, anti).astype(BF16)
    for half in range(2):
        for j in order:
            gather(half, j).wait_send()
            spread(half, j).wait_send()
        for j in far:
            up(half, j).wait_send()
            give_back(half, j).wait_send()
        for j in range(1, ranks):
            share(half, j).wait_send()


def call(kernel, outs, args, scratch=(), far=0, **params):
    whole = pl.BlockSpec(memory_space=pltpu.VMEM)
    return pl.pallas_call(
        kernel,
        out_shape=[jax.ShapeDtypeStruct(shape, dtype) for shape, dtype in outs],
        in_specs=[pl.BlockSpec(memory_space=pltpu.HBM)] * far + [whole] * (len(args) - far),
        out_specs=[whole] * len(outs),
        scratch_shapes=list(scratch),
        compiler_params=pltpu.CompilerParams(vmem_limit_bytes=48 << 20, **params),
    )(*[pltpu.with_memory_space_constraint(a, pltpu.HBM) for a in args[:far]], *args[far:])


def local(hidden, complement, inner, select, step, bias, rate, skip, cot, ccot):
    shards, ranks = lax.axis_size("seq"), lax.axis_size("chan")
    heads = bias.shape[0]
    depth = hidden.shape[1]
    channels = heads * HEAD
    params = jnp.pad(jnp.stack([bias, rate, skip]), ((0, 5), (0, LANES - heads)))
    step = step.T
    send, values, keys, dts, sigs = call(
        project_kernel,
        [
            ((ROW, 2, channels + 8 * heads, STATE), F32),
            ((2 * ROWS, channels), BF16),
            ((2 * ROWS, 2 * STATE), BF16),
            ((2 * ROWS, LANES), F32),
            ((2 * ROWS, LANES), F32),
        ],
        (hidden, complement, inner, select, cot, ccot, step, params),
        [
            pltpu.VMEM((2 * ROWS, depth), BF16),
            pltpu.VMEM((LANES, depth), BF16),
            pltpu.VMEM((ROWS, depth), BF16),
            pltpu.VMEM(inner.shape, BF16),
            pltpu.VMEM(select.shape, BF16),
            pltpu.VMEM(cot.shape, BF16),
            pltpu.VMEM(ccot.shape, BF16),
            pltpu.VMEM(step.shape, BF16),
            pltpu.SemaphoreType.DMA((7,)),
        ],
        far=7,
    )
    layers = shards // ROW
    each = heads // layers
    width = depth // ranks
    dma = lambda *count: pltpu.SemaphoreType.DMA(count)
    wide = lambda *shape: pltpu.VMEM(shape, F32)
    narrow = lambda *shape: pltpu.VMEM(shape, BF16)
    return call(
        functools.partial(main_kernel, layers, ranks),
        [((ROWS, channels), BF16)] * 2 + [((ROWS, width), BF16)] * 2,
        (cot, ccot, inner, select, step, send, values, keys, dts, sigs, params),
        [
            narrow(*cot.shape),
            narrow(*ccot.shape),
            narrow(*inner.shape),
            narrow(*select.shape),
            narrow(*step.shape),
            narrow(LANES, depth),
            wide(ROW, 2, channels, STATE),
            wide(2 * ROWS, channels),
            wide(2 * ROWS, channels),
            wide(2 * ROWS, 2 * STATE),
            wide(2, 2, ROWS, LANES),
            wide(2, ROWS, LANES),
            narrow(2 * ROWS, channels),
            narrow(2 * ROWS, 2 * STATE),
            narrow(2 * ROWS, 2 * STATE),
            narrow(2 * ROWS, LANES),
            narrow(2 * ROWS, LANES),
            wide(*send.shape),
            wide(2, layers, each, HEAD + 8, STATE),
            wide(2, layers, each, HEAD + 8, STATE),
            wide(2, layers, each, HEAD, STATE),
            wide(2, layers, each, HEAD, STATE),
            wide(2, ROW, channels, STATE),
            wide(2, ranks, ROWS, width),
            wide(2, ranks, ROWS, width),
            dma(5),
            dma(2, ROW),
            dma(2, ROW),
            dma(2, layers),
            dma(2, layers),
            dma(2, layers),
            dma(2, layers),
            dma(2, ROW),
            dma(2, ROW),
            dma(2, ranks),
            dma(2, ranks),
        ],
        far=5,
        collective_id=1,
        has_side_effects=True,
    )


def solution(mesh):
    rows = P(("dp", "seq"), None)
    tiles = P(("dp", "seq"), "chan")
    in_specs = (rows, rows, P(None, "chan"), P(), P(None, "chan"), P("chan"), P("chan"), P("chan"), tiles, tiles)
    return jax.shard_map(
        local, mesh=mesh, in_specs=in_specs, out_specs=(tiles,) * 4, check_vma=False
    )
```

time: 210 us -> 148 us (0.70)
  blocking collectives: 149 us -> 0 us
  Pallas kernels: 50.5 us -> 144 us
  local copies, waits for them, and re-layouts: 8.75 us -> 2.57 us
    all_to_all x2 -> x0, blocking collectives: 149 us -> none  [the longest x1 84.8 us: local(): arrived = lax.all_to_all(send, 'seq', 0, 0, tiled=True)]
    pallas_call x4 -> x2, Pallas kernels: 50.5 us -> 144 us  [call(): pl.pallas_call(kernel, out_shape=[jax.ShapeDtypeStruct(shape, dtype) for...]
    unnamed x26 -> x4, local copies, waits for them, and re-layouts: 8.75 us -> 2.57 us
where the time goes in v4:
time: 148 us
  Pallas kernels  144 us (97%)
  local copies, waits for them, and re-layouts  2.57 us (2%)
    pallas_call x2, Pallas kernels, call(): pl.pallas_call(kernel, out_shape=[jax.ShapeDtypeStruct(shape, dtype) for...  144 us

profile of v4, /device:TPU:1, one launch (start us, length us, event | category | flops | bytes accessed | tf_op | source)
XLA Modules:
  0.0 147.6 jit_solution(9904064456265677014)
XLA Ops:
  0.6 0.7 select_maximum_fusion.params
  1.3 6.2 %shard_map.129 = (f32[4,2,576,128]{3,2,1,0:T(8,128)S(1)}, bf16[256,512]{1,0:T(8,128)(2,1)S(1)}, bf16[256,256]{1,0:T(8,128)(2,1)S(1)}, f32[256,128]{1,0:T(8,128)S(1)}, f32[256,128]{1,0:T(8,128)S(1)}) custom-call(bf16[128,2048]{1,0:T(8,128)(2,1)} %hidden_hbm.1, bf16[128,2048]{1,0:T(8,128)(2,1)} %complement_hbm.1, bf16[2048,512]{1,0:T(8,128)(2,1)} %inner_hbm.3, ...), custom_call_target="tpu_custom_call" | custom-call | tf_op jit(solution)/shard_map/pallas_call | solution.py:547
  7.6 137.5 %shard_map.130 = (bf16[128,512]{1,0:T(8,128)(2,1)S(1)}, bf16[128,512]{1,0:T(8,128)(2,1)S(1)}, bf16[128,256]{1,0:T(8,128)(2,1)S(1)}, bf16[128,256]{1,0:T(8,128)(2,1)S(1)}) custom-call(bf16[128,512]{1,0:T(8,128)(2,1)} %cot_hbm.3, bf16[128,512]{1,0:T(8,128)(2,1)} %ccot_hbm.3, bf16[2048,512]{1,0:T(8,128)(2,1)} %inner_hbm.3, bf16[2048,256]{1,0:T(8,128)(2,1)} %select_hbm.3, ...), custom_call_target="tpu_custom_call" | custom-call | tf_op jit(solution)/shard_map/pallas_call | solution.py:547
  145.1 0.7 copy.18
  145.7 0.7 copy.19
  146.4 0.6 copy.20
  147.0 0.6 copy.21

commit v5 on v4

--- a/solution.py
+++ b/solution.py
@@ -72,68 +72,25 @@
     return log_decay, before, upto, total
 
 
-def project_kernel(
-    hidden_hbm,
-    complement_hbm,
-    inner_hbm,
-    select_hbm,
-    cot_hbm,
-    ccot_hbm,
-    step_hbm,
-    params,
-    send,
-    values,
-    keys,
-    dts,
-    sigs,
-    source,
-    step_wide,
-    complement,
-    inner,
-    select,
-    cot,
-    ccot,
-    step,
-    sems,
-):
-    channels = inner.shape[1]
-    heads = channels // HEAD
-    bias, rate = params[0:1, :], params[1:2, :]
-    fetches = [
-        pltpu.make_async_copy(here, there, sems.at[i])
-        for i, (here, there) in enumerate(
-            (
-                (complement_hbm, complement),
-                (hidden_hbm, source.at[:ROWS]),
-                (select_hbm, select),
-                (inner_hbm, inner),
-                (cot_hbm, cot),
-                (ccot_hbm, ccot),
-                (step_hbm, step),
-            )
-        )
-    ]
-    for fetch in fetches:
-        fetch.start()
+def project(fetches, source, complement, inner, select, step, step_wide, params, values, keys, dts, sigs):
+    fetch_complement, fetch_hidden, fetch_step, fetch_select, fetch_inner = fetches
     depth = complement.shape[1]
     blocks = depth // FLIP
     anti = anti_identity()
-    fetches[0].wait()
+    fetch_complement.wait()
     for b in range(blocks):
         block = complement[:, (blocks - 1 - b) * FLIP : (blocks - b) * FLIP]
         source[ROWS:, b * FLIP : (b + 1) * FLIP] = dot(block, anti).astype(BF16)
     step_wide[...] = jnp.zeros_like(step_wide)
-    fetches[6].wait()
-    step_wide[:heads, :] = step[...]
-    fetches[1].wait()
+    fetch_step.wait()
+    step_wide[: step.shape[0], :] = step[...]
+    fetch_hidden.wait()
     src = source[...]
-    raw = dot(src, step_wide[...], 1, 1) + bias
-    fetches[2].wait()
+    raw = dot(src, step_wide[...], 1, 1) + params[0:1, :]
+    fetch_select.wait()
     k_all = dot(src, select[...]).astype(BF16)
-    fetches[3].wait()
+    fetch_inner.wait()
     v_all = dot(src, inner[...]).astype(BF16)
-    fetches[4].wait()
-    fetches[5].wait()
     small = jnp.exp(-jnp.abs(raw))
     one_more = 1.0 + small
     tail = jnp.where(
@@ -144,30 +101,34 @@
     keys[...] = k_all
     dts[...] = dt_all
     sigs[...] = jnp.where(raw >= 0.0, 1.0, small) / one_more
+
+
+def chunk_states(s, values, keys, dts, rate, g_b, send):
+    channels = values.shape[1]
+    heads = channels // HEAD
     spread = spread_matrix(channels)
     ones = jnp.ones((ROWS, STATE), F32)
-    for s in range(2):
-        rows = slice(s * ROWS, (s + 1) * ROWS)
-        dt = dt_all[rows]
-        log_decay, before, upto, total = decay_parts(dt, rate)
-        x = v_all[rows].astype(F32)
-        g = (cot if s == 0 else ccot)[...].astype(F32)
-        write, read = k_all[rows, :STATE], k_all[rows, STATE:]
-        widen = lambda w: dot_left(w, spread)
-        pieces = (
-            (0, 0, widen(jnp.exp(total - upto) * dt) * x, write),
-            (0, 1, widen(jnp.exp(total - before)) * g, read),
-            (1, 0, widen(jnp.exp(before) * dt) * x, write),
-            (1, 1, widen(jnp.exp(upto)) * g, read),
-        )
-        for way, kind, left, right in pieces:
-            state = dot_left(left, right, 0, 0)
-            send[way * 2 + kind, s, :channels, :] = state
-        decay = jnp.exp(dot(log_decay, ones, 0, 0, precision=HIGHEST))
-        for q in range(ROW):
-            for h in range(heads):
-                at = channels + 8 * h
-                send[q, s, at : at + 8, :] = jnp.broadcast_to(decay[h : h + 1], (8, STATE))
+    rows = slice(s * ROWS, (s + 1) * ROWS)
+    dt = dts[rows, :]
+    log_decay, before, upto, total = decay_parts(dt, rate)
+    x = values[rows, :].astype(F32)
+    g = g_b.astype(F32)
+    write, read = keys[rows, :STATE], keys[rows, STATE:]
+    widen = lambda w: dot_left(w, spread)
+    pieces = (
+        (0, 0, widen(jnp.exp(total - upto) * dt) * x, write),
+        (0, 1, widen(jnp.exp(total - before)) * g, read),
+        (1, 0, widen(jnp.exp(before) * dt) * x, write),
+        (1, 1, widen(jnp.exp(upto)) * g, read),
+    )
+    for way, kind, left, right in pieces:
+        state = dot_left(left, right, 0, 0)
+        send[way * 2 + kind, s, :channels, :] = state
+    decay = jnp.exp(dot(log_decay, ones, 0, 0, precision=HIGHEST))
+    for q in range(ROW):
+        for h in range(heads):
+            at = channels + 8 * h
+            send[q, s, at : at + 8, :] = jnp.broadcast_to(decay[h : h + 1], (8, STATE))
 
 
 def within_chunk(s, values, keys, dts, rate, g_b, y_in, d_in, key_in, row_sums, column_sums):
@@ -294,21 +255,25 @@
 def main_kernel(
     layers,
     ranks,
+    complement_hbm,
+    hidden_hbm,
+    step_hbm,
+    select_hbm,
+    inner_hbm,
     cot_hbm,
     ccot_hbm,
-    inner_hbm,
-    select_hbm,
-    step_hbm,
+    params,
+    mixed,
+    cmixed,
+    first,
+    second,
+    complement,
+    source,
     send,
     values,
     keys,
     dts,
     sigs,
-    params,
-    mixed,
-    cmixed,
-    first,
-    second,
     cot,
     ccot,
     inner,
@@ -349,7 +314,15 @@
     fetches = [
         pltpu.make_async_copy(here, there, sems.at[i])
         for i, (here, there) in enumerate(
-            ((cot_hbm, cot), (ccot_hbm, ccot), (inner_hbm, inner), (select_hbm, select), (step_hbm, step))
+            (
+                (complement_hbm, complement),
+                (hidden_hbm, source.at[:ROWS]),
+                (step_hbm, step),
+                (select_hbm, select),
+                (inner_hbm, inner),
+                (cot_hbm, cot),
+                (ccot_hbm, ccot),
+            )
         )
     ]
     for fetch in fetches:
@@ -372,7 +345,7 @@
         pl.semaphore_signal(barrier, inc=1, device_id={"seq": over(j)}, **place)
     for j in range(1, ranks):
         pl.semaphore_signal(barrier, inc=1, device_id={"chan": across(j)}, **place)
-    pl.semaphore_wait(barrier, ROW + layers + ranks - 3)
+    project(fetches[:5], source, complement, inner, select, step, step_wide, params, values, keys, dts, sigs)
 
     def copy(here, there, sent, got, device):
         return pltpu.make_async_remote_copy(
@@ -405,18 +378,17 @@
 
     order = (1, 3, 2)
     far = tuple(j for j in (1, 7, 2, 6, 3, 5, 4) if j < layers)
-    for half in range(2):
+    for s, g in ((0, cot), (1, ccot)):
+        fetches[5 + s].wait()
+        chunk_states(s, values, keys, dts, params[1:2, :], g[...], send)
+        if s == 0:
+            pl.semaphore_wait(barrier, ROW + layers + ranks - 3)
         for j in order:
-            gather(half, j).start()
+            gather(s, j).start()
     rows_in[member] = send[member]
     column_sums[...] = jnp.zeros_like(column_sums)
-    step_wide[...] = jnp.zeros_like(step_wide)
     for s, g in ((0, cot), (1, ccot)):
-        fetches[s].wait()
         within_chunk(s, values, keys, dts, params[1:2, :], g[...], y_in, d_in, key_in, row_sums, column_sums)
-    for fetch in fetches[2:]:
-        fetch.wait()
-    step_wide[:heads, :] = step[...]
     zero = jnp.zeros((HEAD // 8, 8, STATE), F32)
 
     def part(source, h, half):
@@ -561,29 +533,6 @@
     channels = heads * HEAD
     params = jnp.pad(jnp.stack([bias, rate, skip]), ((0, 5), (0, LANES - heads)))
     step = step.T
-    send, values, keys, dts, sigs = call(
-        project_kernel,
-        [
-            ((ROW, 2, channels + 8 * heads, STATE), F32),
-            ((2 * ROWS, channels), BF16),
-            ((2 * ROWS, 2 * STATE), BF16),
-            ((2 * ROWS, LANES), F32),
-            ((2 * ROWS, LANES), F32),
-        ],
-        (hidden, complement, inner, select, cot, ccot, step, params),
-        [
-            pltpu.VMEM((2 * ROWS, depth), BF16),
-            pltpu.VMEM((LANES, depth), BF16),
-            pltpu.VMEM((ROWS, depth), BF16),
-            pltpu.VMEM(inner.shape, BF16),
-            pltpu.VMEM(select.shape, BF16),
-            pltpu.VMEM(cot.shape, BF16),
-            pltpu.VMEM(ccot.shape, BF16),
-            pltpu.VMEM(step.shape, BF16),
-            pltpu.SemaphoreType.DMA((7,)),
-        ],
-        far=7,
-    )
     layers = shards // ROW
     each = heads // layers
     width = depth // ranks
@@ -593,8 +542,15 @@
     return call(
         functools.partial(main_kernel, layers, ranks),
         [((ROWS, channels), BF16)] * 2 + [((ROWS, width), BF16)] * 2,
-        (cot, ccot, inner, select, step, send, values, keys, dts, sigs, params),
+        (complement, hidden, step, select, inner, cot, ccot, params),
         [
+            narrow(ROWS, depth),
+            narrow(2 * ROWS, depth),
+            wide(ROW, 2, channels + 8 * heads, STATE),
+            narrow(2 * ROWS, channels),
+            narrow(2 * ROWS, 2 * STATE),
+            wide(2 * ROWS, LANES),
+            wide(2 * ROWS, LANES),
             narrow(*cot.shape),
             narrow(*ccot.shape),
             narrow(*inner.shape),
@@ -612,7 +568,7 @@
             narrow(2 * ROWS, 2 * STATE),
             narrow(2 * ROWS, LANES),
             narrow(2 * ROWS, LANES),
-            wide(*send.shape),
+            wide(ROW, 2, channels + 8 * heads, STATE),
             wide(2, layers, each, HEAD + 8, STATE),
             wide(2, layers, each, HEAD + 8, STATE),
             wide(2, layers, each, HEAD, STATE),
@@ -620,7 +576,7 @@
             wide(2, ROW, channels, STATE),
             wide(2, ranks, ROWS, width),
             wide(2, ranks, ROWS, width),
-            dma(5),
+            dma(7),
             dma(2, ROW),
             dma(2, ROW),
             dma(2, layers),
@@ -632,7 +588,7 @@
             dma(2, ranks),
             dma(2, ranks),
         ],
-        far=5,
+        far=7,
         collective_id=1,
         has_side_effects=True,
     )

time: 148 us -> 139 us (0.939); the launches traced: 148 us -> 136 us
  Pallas kernels: 144 us -> 132 us
    pallas_call x2 -> x1, Pallas kernels: 144 us -> 132 us  [call(): pl.pallas_call(kernel, out_shape=[jax.ShapeDtypeStruct(shape, dtype) for...]
where the time goes in v5:
time: 139 us; the launch traced here: 136 us
  Pallas kernels  132 us (95%)
  local copies, waits for them, and re-layouts  2.57 us (2%)
    pallas_call x1, Pallas kernels, call(): pl.pallas_call(kernel, out_shape=[jax.ShapeDtypeStruct(shape, dtype) for...  132 us

profile of v5, /device:TPU:1, one launch (start us, length us, event | category | flops | bytes accessed | tf_op | source)
XLA Modules:
  0.0 136.4 jit_solution(17161678152017160494)
XLA Ops:
  0.6 0.7 select_maximum_fusion.params
  1.3 132.5 %shard_map.129 = (bf16[128,512]{1,0:T(8,128)(2,1)S(1)}, bf16[128,512]{1,0:T(8,128)(2,1)S(1)}, bf16[128,256]{1,0:T(8,128)(2,1)S(1)}, bf16[128,256]{1,0:T(8,128)(2,1)S(1)}) custom-call(bf16[128,2048]{1,0:T(8,128)(2,1)} %complement_hbm.1, bf16[128,2048]{1,0:T(8,128)(2,1)} %hidden_hbm.1, bf16[8,2048]{1,0:T(8,128)(2,1)} %bitcast.4, bf16[2048,256]{1,0:T(8,128)(2,1)} %select_hbm.1, ...), custom_call_target="tpu_custom_call" | custom-call | tf_op jit(solution)/shard_map/pallas_call | solution.py:519
  133.8 0.7 copy.18
  134.5 0.7 copy.19
  135.1 0.6 copy.20
  135.7 0.6 copy.21

commit v6 on v5

--- a/solution.py
+++ b/solution.py
@@ -39,8 +39,8 @@
     return dot(a, high, ca, cb) + dot(a, low, ca, cb)
 
 
-def dot_both(a, b, ca=1, cb=0):
-    a_high, a_low = split(a)
+def dot_terms(a, b, ca=1, cb=0):
+    a_high, a_low = a
     b_high, b_low = split(b)
     return dot(a_high, b_high, ca, cb) + (dot(a_high, b_low, ca, cb) + dot(a_low, b_high, ca, cb))
 
@@ -190,6 +190,7 @@
 
 def finish(
     s,
+    wait,
     entry,
     values,
     keys,
@@ -225,13 +226,16 @@
     u_fwd, u_bwd = widen(jnp.exp(total - upto)), widen(jnp.exp(before))
     w_fwd, w_bwd = widen(jnp.exp(upto)), widen(jnp.exp(total - before))
     dt_wide = widen(dt)
+    w_g_fwd, w_g_bwd = split(w_fwd * g), split(w_bwd * g)
+    u_x_fwd, u_x_bwd = split(u_fwd * dt_wide * x), split(u_bwd * dt_wide * x)
+    wait()
     h_in, m_in, k_in, l_in = entry[0, s], entry[1, s], entry[2, s], entry[3, s]
     y_fwd = w_fwd * dot_right(read, h_in, 1, 1)
     y_bwd = w_bwd * dot_right(read, k_in, 1, 1)
     x_l = u_fwd * dot_right(write, l_in, 1, 1)
     x_m = u_bwd * dot_right(write, m_in, 1, 1)
-    d_read = dot_both(w_fwd * g, h_in) + dot_both(w_bwd * g, k_in)
-    d_write = dot_both(u_fwd * dt_wide * x, l_in) + dot_both(u_bwd * dt_wide * x, m_in)
+    d_read = dot_terms(w_g_fwd, h_in) + dot_terms(w_g_bwd, k_in)
+    d_write = dot_terms(u_x_fwd, l_in) + dot_terms(u_x_bwd, m_in)
     r_fwd, r_bwd = narrow(g * y_fwd), narrow(g * y_bwd)
     q_fwd, q_bwd = narrow(x * x_l), narrow(x * x_m)
     both = dot_right(spread, l_in * h_in + m_in * k_in)
@@ -461,10 +465,14 @@
         return value + (dot(d_raw_high[rows, :], steps) + dot(d_raw_low[rows, :], steps))
 
     for s, g, out in ((0, cot, mixed), (1, ccot, cmixed)):
-        for j in order:
-            spread(s, j).wait_recv()
+
+        def settled():
+            for j in order:
+                spread(s, j).wait_recv()
+
         finish(
             s,
+            settled,
             entry,
             values,
             keys,

time: 139 us -> 139 us (level)
  no operation moved by 1% of the time
where the time goes in v6:
time: 139 us; the launch traced here: 136 us
  Pallas kernels  132 us (95%)
  local copies, waits for them, and re-layouts  2.57 us (2%)
    pallas_call x1, Pallas kernels, call(): pl.pallas_call(kernel, out_shape=[jax.ShapeDtypeStruct(shape, dtype) for...  132 us

profile of v6, /device:TPU:1, one launch (start us, length us, event | category | flops | bytes accessed | tf_op | source)
XLA Modules:
  0.0 136.4 jit_solution(17393502293389290220)
XLA Ops:
  0.6 0.7 select_maximum_fusion.params
  1.3 132.5 %shard_map.129 = (bf16[128,512]{1,0:T(8,128)(2,1)S(1)}, bf16[128,512]{1,0:T(8,128)(2,1)S(1)}, bf16[128,256]{1,0:T(8,128)(2,1)S(1)}, bf16[128,256]{1,0:T(8,128)(2,1)S(1)}) custom-call(bf16[128,2048]{1,0:T(8,128)(2,1)} %complement_hbm.1, bf16[128,2048]{1,0:T(8,128)(2,1)} %hidden_hbm.1, bf16[8,2048]{1,0:T(8,128)(2,1)} %bitcast.4, bf16[2048,256]{1,0:T(8,128)(2,1)} %select_hbm.1, ...), custom_call_target="tpu_custom_call" | custom-call | tf_op jit(solution)/shard_map/pallas_call | solution.py:527
  133.8 0.7 copy.18
  134.5 0.7 copy.19
  135.1 0.6 copy.20
  135.7 0.6 copy.21

commit v7 on v5

--- a/solution.py
+++ b/solution.py
@@ -376,7 +376,7 @@
         there = shares.at[half, rank]
         return copy(term.at[half, across(j)], there, share_out.at[half, j], share_in.at[half, j], {"chan": across(j)})
 
-    order = (1, 3, 2)
+    order = (2, 1, 3)
     far = tuple(j for j in (1, 7, 2, 6, 3, 5, 4) if j < layers)
     for s, g in ((0, cot), (1, ccot)):
         fetches[5 + s].wait()

time: 139 us -> 143 us (1.029)
  the two profiles are of different devices: /device:TPU:1 before, /device:TPU:42 now
where the time goes in v7:
time: 143 us; the launch traced here: 142 us
  Pallas kernels  139 us (97%)
  local copies, waits for them, and re-layouts  2.57 us (2%)
    pallas_call x1, Pallas kernels, call(): pl.pallas_call(kernel, out_shape=[jax.ShapeDtypeStruct(shape, dtype) for...  139 us

profile of v7, /device:TPU:42, one launch (start us, length us, event | category | flops | bytes accessed | tf_op | source)
XLA Modules:
  0.0 142.5 jit_solution(15006161054960197833)
XLA Ops:
  0.6 0.7 select_maximum_fusion.params
  1.3 138.6 %shard_map.129 = (bf16[128,512]{1,0:T(8,128)(2,1)S(1)}, bf16[128,512]{1,0:T(8,128)(2,1)S(1)}, bf16[128,256]{1,0:T(8,128)(2,1)S(1)}, bf16[128,256]{1,0:T(8,128)(2,1)S(1)}) custom-call(bf16[128,2048]{1,0:T(8,128)(2,1)} %complement_hbm.1, bf16[128,2048]{1,0:T(8,128)(2,1)} %hidden_hbm.1, bf16[8,2048]{1,0:T(8,128)(2,1)} %bitcast.4, bf16[2048,256]{1,0:T(8,128)(2,1)} %select_hbm.1, ...), custom_call_target="tpu_custom_call" | custom-call | tf_op jit(solution)/shard_map/pallas_call | solution.py:519
  139.9 0.7 copy.18
  140.6 0.7 copy.19
  141.2 0.6 copy.20
  141.9 0.6 copy.21
